TPU v7x, 512 devices: a whole 4x8x8 slice. The times are simulated.
512 devices in a mesh: cell: 128 (over z, y, core), tm: 4 (over x).
Axes of the slice: x: 4, y: 8, z: 8, core: 2. Of those that a mesh axis runs over, the one named last changes fastest.
Arguments:
- snapshots: float32 [384, 5, 98304], P('tm', None, 'cell'), may hold values from -6 to 6
- volumes: float32 [98304], P('cell'), may hold values from 0.1 to 10
- freq_index: int32 [8], replicated, may hold values from 1 to 63, as said below
- block_start: int32 [5], replicated, may hold values from 0 to 256, as said below
Outputs:
- modes: float32 [8, 10, 5, 98304], P('tm', None, None, 'cell')
- triangle: float32 [8, 10, 10], P('tm')
Inputs may be any that keep to these rules, and one draw needn't show every extreme that they name: `freq_index`: distinct indices; the smallest and the largest allowed value both occur. `block_start`: rising; the first is 0 and the last is 256; with s = 64, start b lies within s // 4 of b * s.
All inputs are finite; a program needn't handle non-finite values.
Results may differ from a plain program's by a relative error of at most 0.000078.
Values sent between devices are 32-bit elements; how exact they have to be, the bound alone decides.
No kernel may reach another device: no remote copies, remote signals or barrier semaphores. Data moves between devices by JAX's collectives and lax.ppermute only.
A program may use at most 64 MiB of HBM per device.

v0:
```python
import jax
import jax.numpy as jnp
from jax import lax
from jax.sharding import PartitionSpec as P

NFFT = 128
NF = 8
NB = 5


def partner_2(block, axis, distance):
    count = lax.axis_size(axis)
    route = []
    for low in range(count):
        high = low | 1 << distance
        if high != low and high < count:
            route += [(low, high), (high, low)]
    return lax.ppermute(block, axis, route)


def make_table(freq_index, block_start, times):
    tau = times[None, :] - block_start[:, None]
    valid = (tau >= 0) & (tau < NFFT)
    tauf = tau.astype(jnp.float32)
    hann = jnp.where(valid, 0.5 - 0.5 * jnp.cos(2.0 * jnp.pi * tauf / NFFT), 0.0)
    phase = jnp.mod(freq_index[:, None, None] * tau[None, :, :], NFFT).astype(jnp.float32)
    angle = 2.0 * jnp.pi * phase / NFFT
    real_part = hann[None] * jnp.cos(angle)
    imag_part = -hann[None] * jnp.sin(angle)
    table = jnp.stack([real_part, imag_part], axis=1)
    return table.reshape(NF * 2 * NB, times.shape[0])


def outer_sum(lower_a, lower_b):
    first = jnp.einsum("frk,fsk->frs", lower_a, lower_a, precision=lax.Precision.HIGHEST)
    second = jnp.einsum("frk,fsk->frs", lower_b, lower_b, precision=lax.Precision.HIGHEST)
    return first + second


def on_device(snapshots, volumes, freq_index, block_start):
    tdev, nvar, cells = snapshots.shape
    tm_count = lax.axis_size("tm")
    cell_count = lax.axis_size("cell")
    fdev = NF // tm_count
    columns = 2 * NB
    regrouped = lax.all_to_all(snapshots, "tm", split_axis=2, concat_axis=0, tiled=True)
    total_time = regrouped.shape[0]
    quarter = regrouped.shape[2]
    times = jnp.arange(total_time, dtype=jnp.int32)
    table = make_table(freq_index, block_start, times)
    flat = regrouped.reshape(total_time, nvar * quarter)
    local_spec = jnp.dot(
        table, flat, precision=lax.Precision.HIGHEST, preferred_element_type=jnp.float32
    )
    local_spec = local_spec.reshape(NF * columns, nvar, quarter)
    spectra = lax.all_to_all(local_spec, "tm", split_axis=0, concat_axis=2, tiled=True)
    spectra = spectra.reshape(fdev, columns, nvar, cells)
    weighted = spectra * jnp.sqrt(volumes)[None, None, None, :]
    weighted = weighted.reshape(fdev, columns, nvar * cells)
    gram_local = jnp.einsum("frc,fsc->frs", weighted, weighted, precision=lax.Precision.HIGHEST)
    lower = jnp.linalg.cholesky(gram_local)
    for bit in range(cell_count.bit_length() - 1):
        partner = partner_2(lower, "cell", bit)
        lower = jnp.linalg.cholesky(outer_sum(lower, partner))
    solved = jax.vmap(lambda a, b: jax.scipy.linalg.solve_triangular(a, b, lower=True))(
        lower, weighted
    )
    total_rows = nvar * cells * cell_count
    modes = (jnp.sqrt(jnp.float32(total_rows)) * solved).reshape(fdev, columns, nvar, cells)
    triangle = jnp.transpose(lower, (0, 2, 1)) / jnp.sqrt(jnp.float32(total_rows * NFFT))
    return (modes, triangle)


def solution(mesh):
    placed = (P("tm", None, "cell"), P("cell"), P(), P())
    return jax.shard_map(
        on_device,
        mesh=mesh,
        in_specs=placed,
        out_specs=(P("tm", None, None, "cell"), P("tm", None, None)),
        check_vma=False,
    )
```

profile of v0, /device:TPU:40, one launch (start us, length us, event | category | flops | bytes accessed | tf_op | source)
XLA Modules:
  0.0 134.1 jit_solution(7466933497148265520)
XLA Ops:
  0.6 2.3 %copy.92 = f32[96,5,768]{0,1,2:T(8,128)S(1)} copy(f32[96,5,768]{2,0,1:T(8,128)} %param.5) | data formatting | bytes 2949120 | tf_op args[0]
  3.0 3.5 %reshape.153 = f32[4,1,92160]{2,1,0:T(1,128)} reshape(f32[768,5,96]{2,1,0:T(8,128)S(1)} %bitcast.84) | data formatting | bytes 2949120
  6.4 4.4 %all-to-all-start = ((f32[4,1,92160]{2,1,0:T(1,128)}), f32[4,1,92160]{2,1,0:T(1,128)S(1)}, u32[]{:S(2)}, u32[]{:S(2)}) async-start(f32[4,1,92160]{2,1,0:T(1,128)} %reshape.153), calls=%async_computation | async-start | bytes 2949120 | tf_op jit(solution)/shard_map/all_to_all | solution.py:46
  11.6 18.9 %all-to-all-done = f32[4,1,92160]{2,1,0:T(1,128)S(1)} async-done(((f32[4,1,92160]{2,1,0:T(1,128)}), f32[4,1,92160]{2,1,0:T(1,128)S(1)}, u32[]{:S(2)}, u32[]{:S(2)}) %all-to-all-start) | async-done | bytes 1474592 | tf_op jit(solution)/shard_map/all_to_all | solution.py:46
  31.0 6.1 %reduce.4 = f32[4,92160]{1,0:T(4,128)} reduce(f32[4,1,92160]{2,1,0:T(1,128)S(1)} %all-to-all-done, f32[]{:T(128)} %broadcast.245), dimensions={1}, to_apply=%all_to_all.22.reduce_sub_computation | reduce | bytes 2949124 | tf_op jit(solution)/shard_map/all_to_all | solution.py:46
  37.1 3.0 %reshape.154 = f32[768,5,96]{2,1,0:T(8,128)S(1)} reshape(f32[4,92160]{1,0:T(4,128)} %reduce.4) | data formatting | bytes 2949120
  40.1 2.6 %copy.93 = f32[4,96,5,192]{1,0,3,2:T(4,128)} copy(f32[4,96,5,192]{1,2,3,0:T(8,128)S(1)} %bitcast.83) | data formatting | bytes 2949120 | tf_op jit(solution)/shard_map/all_to_all | solution.py:46
  42.7 2.3 %reshape.147 = f32[384,960]{0,1:T(8,128)S(1)} reshape(f32[4,96,5,192]{1,0,3,2:T(4,128)} %copy.93) | data formatting | bytes 2949120 | tf_op jit(solution)/shard_map/reshape | solution.py:51
  44.9 2.0 %fusion.21 = f32[80,5,192]{2,0,1:T(8,128)S(1)} fusion(f32[80,384,1]{1,0,2:T(8,128)S(1)} %reshape.150, f32[5,192,384]{2,1,0:T(8,128)S(1)} %bitcast.85), kind=kOutput, calls=%fused_computation.75 | convolution fusion | flops 353894400 | bytes 1904640 | tf_op jit(solution)/shard_map/dot_general | solution.py:52
  48.4 3.6 %all-to-all-start.1 = ((f32[4,1,19200]{2,1,0:T(1,128)}), f32[4,1,19200]{2,1,0:T(1,128)S(1)}, u32[]{:S(2)}, u32[]{:S(2)}) async-start(f32[4,1,19200]{2,1,0:T(1,128)} %reshape.155), calls=%async_computation.1 | async-start | bytes 614400 | tf_op jit(solution)/shard_map/all_to_all | solution.py:56
  52.1 6.6 %all-to-all-done.1 = f32[4,1,19200]{2,1,0:T(1,128)S(1)} async-done(((f32[4,1,19200]{2,1,0:T(1,128)}), f32[4,1,19200]{2,1,0:T(1,128)S(1)}, u32[]{:S(2)}, u32[]{:S(2)}) %all-to-all-start.1) | async-done | bytes 307232 | tf_op jit(solution)/shard_map/all_to_all | solution.py:56
  62.1 1.8 %custom-call.15 = f32[2,10,10]{2,1,0:T(8,128)S(1)} custom-call(f32[2,10,10]{2,1,0:T(8,128)S(1)} %fusion.16), custom_call_target="Cholesky" | custom-call | tf_op jit(solution)/shard_map/jit(cholesky)/cholesky | solution.py:61
  64.2 1.9 %collective-permute-start = (f32[2,10,10]{2,1,0:T(8,128)S(1)}, f32[2,10,10]{2,1,0:T(8,128)S(1)}, u32[]{:S(2)}, u32[]{:S(2)}) collective-permute-start(f32[2,10,10]{2,1,0:T(8,128)S(1)} %select_select_fusion.7), channel_id=1, source_target_pairs={{0,4},{4,0},{8,12},{12,8},{16,20},{20,16},{24,28},{28,24},{32,36},... | collective-permute-start | bytes 2408 | tf_op jit(solution)/shard_map/ppermute | solution.py:18
  67.5 1.8 %custom-call.16 = f32[2,10,10]{2,1,0:T(8,128)S(1)} custom-call(f32[2,10,10]{2,1,0:T(8,128)S(1)} %fusion.15), custom_call_target="Cholesky" | custom-call | tf_op jit(solution)/shard_map/jit(cholesky)/cholesky | solution.py:64
  69.6 3.3 %collective-permute-start.1 = (f32[2,10,10]{2,1,0:T(8,128)S(1)}, f32[2,10,10]{2,1,0:T(8,128)S(1)}, u32[]{:S(2)}, u32[]{:S(2)}) collective-permute-start(f32[2,10,10]{2,1,0:T(8,128)S(1)} %select_select_fusion.6), channel_id=1, source_target_pairs={{0,8},{8,0},{4,12},{12,4},{16,24},{24,16},{20,28},{28,20},{32,40},... | collective-permute-start | bytes 2408 | tf_op jit(solution)/shard_map/ppermute | solution.py:18
  73.0 2.2 %collective-permute-done.1 = f32[2,10,10]{2,1,0:T(8,128)S(1)} collective-permute-done((f32[2,10,10]{2,1,0:T(8,128)S(1)}, f32[2,10,10]{2,1,0:T(8,128)S(1)}, u32[]{:S(2)}, u32[]{:S(2)}) %collective-permute-start.1) | collective-permute-done | bytes 832 | tf_op jit(solution)/shard_map/ppermute | solution.py:18
  75.5 1.8 %custom-call.17 = f32[2,10,10]{2,1,0:T(8,128)S(1)} custom-call(f32[2,10,10]{2,1,0:T(8,128)S(1)} %fusion.14), custom_call_target="Cholesky" | custom-call | tf_op jit(solution)/shard_map/jit(cholesky)/cholesky | solution.py:64
  77.6 2.7 %collective-permute-start.2 = (f32[2,10,10]{2,1,0:T(8,128)S(1)}, f32[2,10,10]{2,1,0:T(8,128)S(1)}, u32[]{:S(2)}, u32[]{:S(2)}) collective-permute-start(f32[2,10,10]{2,1,0:T(8,128)S(1)} %select_select_fusion.5), channel_id=1, source_target_pairs={{0,16},{16,0},{4,20},{20,4},{8,24},{24,8},{12,28},{28,12},{32,48},... | collective-permute-start | bytes 2408 | tf_op jit(solution)/shard_map/ppermute | solution.py:18
  80.4 3.7 %collective-permute-done.2 = f32[2,10,10]{2,1,0:T(8,128)S(1)} collective-permute-done((f32[2,10,10]{2,1,0:T(8,128)S(1)}, f32[2,10,10]{2,1,0:T(8,128)S(1)}, u32[]{:S(2)}, u32[]{:S(2)}) %collective-permute-start.2) | collective-permute-done | bytes 832 | tf_op jit(solution)/shard_map/ppermute | solution.py:18
  84.4 1.8 %custom-call.18 = f32[2,10,10]{2,1,0:T(8,128)S(1)} custom-call(f32[2,10,10]{2,1,0:T(8,128)S(1)} %fusion.13), custom_call_target="Cholesky" | custom-call | tf_op jit(solution)/shard_map/jit(cholesky)/cholesky | solution.py:64
  86.5 2.9 %collective-permute-start.3 = (f32[2,10,10]{2,1,0:T(8,128)S(1)}, f32[2,10,10]{2,1,0:T(8,128)S(1)}, u32[]{:S(2)}, u32[]{:S(2)}) collective-permute-start(f32[2,10,10]{2,1,0:T(8,128)S(1)} %select_select_fusion.4), channel_id=1, source_target_pairs={{0,32},{32,0},{4,36},{36,4},{8,40},{40,8},{12,44},{44,12},{16,48},... | collective-permute-start | bytes 2408 | tf_op jit(solution)/shard_map/ppermute | solution.py:18
  89.5 6.6 %collective-permute-done.3 = f32[2,10,10]{2,1,0:T(8,128)S(1)} collective-permute-done((f32[2,10,10]{2,1,0:T(8,128)S(1)}, f32[2,10,10]{2,1,0:T(8,128)S(1)}, u32[]{:S(2)}, u32[]{:S(2)}) %collective-permute-start.3) | collective-permute-done | bytes 832 | tf_op jit(solution)/shard_map/ppermute | solution.py:18
  96.3 1.8 %custom-call.19 = f32[2,10,10]{2,1,0:T(8,128)S(1)} custom-call(f32[2,10,10]{2,1,0:T(8,128)S(1)} %fusion.12), custom_call_target="Cholesky" | custom-call | tf_op jit(solution)/shard_map/jit(cholesky)/cholesky | solution.py:64
  98.3 4.3 %collective-permute-start.4 = (f32[2,10,10]{2,1,0:T(8,128)S(1)}, f32[2,10,10]{2,1,0:T(8,128)S(1)}, u32[]{:S(2)}, u32[]{:S(2)}) collective-permute-start(f32[2,10,10]{2,1,0:T(8,128)S(1)} %select_select_fusion.3), channel_id=1, source_target_pairs={{0,64},{64,0},{4,68},{68,4},{8,72},{72,8},{12,76},{76,12},{16,80},... | collective-permute-start | bytes 2408 | tf_op jit(solution)/shard_map/ppermute | solution.py:18
  102.8 1.6 %collective-permute-done.4 = f32[2,10,10]{2,1,0:T(8,128)S(1)} collective-permute-done((f32[2,10,10]{2,1,0:T(8,128)S(1)}, f32[2,10,10]{2,1,0:T(8,128)S(1)}, u32[]{:S(2)}, u32[]{:S(2)}) %collective-permute-start.4) | collective-permute-done | bytes 832 | tf_op jit(solution)/shard_map/ppermute | solution.py:18
  104.6 1.8 %custom-call.20 = f32[2,10,10]{2,1,0:T(8,128)S(1)} custom-call(f32[2,10,10]{2,1,0:T(8,128)S(1)} %fusion.11), custom_call_target="Cholesky" | custom-call | tf_op jit(solution)/shard_map/jit(cholesky)/cholesky | solution.py:64
  106.7 6.1 %collective-permute-start.5 = (f32[2,10,10]{2,1,0:T(8,128)S(1)}, f32[2,10,10]{2,1,0:T(8,128)S(1)}, u32[]{:S(2)}, u32[]{:S(2)}) collective-permute-start(f32[2,10,10]{2,1,0:T(8,128)S(1)} %select_select_fusion.2), channel_id=1, source_target_pairs={{0,128},{128,0},{4,132},{132,4},{8,136},{136,8},{12,140},{140,12},... | collective-permute-start | bytes 2408 | tf_op jit(solution)/shard_map/ppermute | solution.py:18
  112.9 1.6 %collective-permute-done.5 = f32[2,10,10]{2,1,0:T(8,128)S(1)} collective-permute-done((f32[2,10,10]{2,1,0:T(8,128)S(1)}, f32[2,10,10]{2,1,0:T(8,128)S(1)}, u32[]{:S(2)}, u32[]{:S(2)}) %collective-permute-start.5) | collective-permute-done | bytes 832 | tf_op jit(solution)/shard_map/ppermute | solution.py:18
  114.7 1.8 %custom-call.21 = f32[2,10,10]{2,1,0:T(8,128)S(1)} custom-call(f32[2,10,10]{2,1,0:T(8,128)S(1)} %fusion.10), custom_call_target="Cholesky" | custom-call | tf_op jit(solution)/shard_map/jit(cholesky)/cholesky | solution.py:64
  116.8 9.3 %collective-permute-start.6 = (f32[2,10,10]{2,1,0:T(8,128)S(1)}, f32[2,10,10]{2,1,0:T(8,128)S(1)}, u32[]{:S(2)}, u32[]{:S(2)}) collective-permute-start(f32[2,10,10]{2,1,0:T(8,128)S(1)} %select_select_fusion.1), channel_id=1, source_target_pairs={{0,256},{256,0},{4,260},{260,4},{8,264},{264,8},{12,268},{268,12},... | collective-permute-start | bytes 2408 | tf_op jit(solution)/shard_map/ppermute | solution.py:18
  126.2 1.6 %collective-permute-done.6 = f32[2,10,10]{2,1,0:T(8,128)S(1)} collective-permute-done((f32[2,10,10]{2,1,0:T(8,128)S(1)}, f32[2,10,10]{2,1,0:T(8,128)S(1)}, u32[]{:S(2)}, u32[]{:S(2)}) %collective-permute-start.6) | collective-permute-done | bytes 832 | tf_op jit(solution)/shard_map/ppermute | solution.py:18
  128.1 1.8 %custom-call.22 = f32[2,10,10]{2,1,0:T(8,128)S(1)} custom-call(f32[2,10,10]{2,1,0:T(8,128)S(1)} %fusion.9), custom_call_target="Cholesky" | custom-call | tf_op jit(solution)/shard_map/jit(cholesky)/cholesky | solution.py:64
  (84 shorter events, 15.8 us)
Async XLA Ops:
  6.4 4.4 %copy-start.1 = (s32[5]{0:T(128)S(1)}, s32[5]{0:T(128)}, u32[]{:S(2)}) copy-start(s32[5]{0:T(128)} %param.8) | copy-start | bytes 64
  6.4 4.6 %copy-start.2 = (s32[8]{0:T(128)S(1)}, s32[8]{0:T(128)}, u32[]{:S(2)}) copy-start(s32[8]{0:T(128)} %param.7) | copy-start | bytes 100
  6.4 24.1 %all-to-all-start = ((f32[4,1,92160]{2,1,0:T(1,128)}), f32[4,1,92160]{2,1,0:T(1,128)S(1)}, u32[]{:S(2)}, u32[]{:S(2)}) async-start(f32[4,1,92160]{2,1,0:T(1,128)} %reshape.153), calls=%async_computation | async-start | bytes 2949120 | tf_op jit(solution)/shard_map/all_to_all | solution.py:46
  47.0 5.1 %copy-start = (f32[768]{0:T(1024)S(1)}, f32[768]{0:T(1024)}, u32[]{:S(2)}) copy-start(f32[768]{0:T(1024)} %param.6) | copy-start | bytes 9220
  48.4 10.3 %all-to-all-start.1 = ((f32[4,1,19200]{2,1,0:T(1,128)}), f32[4,1,19200]{2,1,0:T(1,128)S(1)}, u32[]{:S(2)}, u32[]{:S(2)}) async-start(f32[4,1,19200]{2,1,0:T(1,128)} %reshape.155), calls=%async_computation.1 | async-start | bytes 614400 | tf_op jit(solution)/shard_map/all_to_all | solution.py:56
  64.2 3.1 %collective-permute-start = (f32[2,10,10]{2,1,0:T(8,128)S(1)}, f32[2,10,10]{2,1,0:T(8,128)S(1)}, u32[]{:S(2)}, u32[]{:S(2)}) collective-permute-start(f32[2,10,10]{2,1,0:T(8,128)S(1)} %select_select_fusion.7), channel_id=1, source_target_pairs={{0,4},{4,0},{8,12},{12,8},{16,20},{20,16},{24,28},{28,24},{32,36},... | collective-permute-start | bytes 2408 | tf_op jit(solution)/shard_map/ppermute | solution.py:18
  69.6 5.6 %collective-permute-start.1 = (f32[2,10,10]{2,1,0:T(8,128)S(1)}, f32[2,10,10]{2,1,0:T(8,128)S(1)}, u32[]{:S(2)}, u32[]{:S(2)}) collective-permute-start(f32[2,10,10]{2,1,0:T(8,128)S(1)} %select_select_fusion.6), channel_id=1, source_target_pairs={{0,8},{8,0},{4,12},{12,4},{16,24},{24,16},{20,28},{28,20},{32,40},... | collective-permute-start | bytes 2408 | tf_op jit(solution)/shard_map/ppermute | solution.py:18
  77.6 6.6 %collective-permute-start.2 = (f32[2,10,10]{2,1,0:T(8,128)S(1)}, f32[2,10,10]{2,1,0:T(8,128)S(1)}, u32[]{:S(2)}, u32[]{:S(2)}) collective-permute-start(f32[2,10,10]{2,1,0:T(8,128)S(1)} %select_select_fusion.5), channel_id=1, source_target_pairs={{0,16},{16,0},{4,20},{20,4},{8,24},{24,8},{12,28},{28,12},{32,48},... | collective-permute-start | bytes 2408 | tf_op jit(solution)/shard_map/ppermute | solution.py:18
  86.5 9.6 %collective-permute-start.3 = (f32[2,10,10]{2,1,0:T(8,128)S(1)}, f32[2,10,10]{2,1,0:T(8,128)S(1)}, u32[]{:S(2)}, u32[]{:S(2)}) collective-permute-start(f32[2,10,10]{2,1,0:T(8,128)S(1)} %select_select_fusion.4), channel_id=1, source_target_pairs={{0,32},{32,0},{4,36},{36,4},{8,40},{40,8},{12,44},{44,12},{16,48},... | collective-permute-start | bytes 2408 | tf_op jit(solution)/shard_map/ppermute | solution.py:18
  98.3 6.0 %collective-permute-start.4 = (f32[2,10,10]{2,1,0:T(8,128)S(1)}, f32[2,10,10]{2,1,0:T(8,128)S(1)}, u32[]{:S(2)}, u32[]{:S(2)}) collective-permute-start(f32[2,10,10]{2,1,0:T(8,128)S(1)} %select_select_fusion.3), channel_id=1, source_target_pairs={{0,64},{64,0},{4,68},{68,4},{8,72},{72,8},{12,76},{76,12},{16,80},... | collective-permute-start | bytes 2408 | tf_op jit(solution)/shard_map/ppermute | solution.py:18
  106.7 7.8 %collective-permute-start.5 = (f32[2,10,10]{2,1,0:T(8,128)S(1)}, f32[2,10,10]{2,1,0:T(8,128)S(1)}, u32[]{:S(2)}, u32[]{:S(2)}) collective-permute-start(f32[2,10,10]{2,1,0:T(8,128)S(1)} %select_select_fusion.2), channel_id=1, source_target_pairs={{0,128},{128,0},{4,132},{132,4},{8,136},{136,8},{12,140},{140,12},... | collective-permute-start | bytes 2408 | tf_op jit(solution)/shard_map/ppermute | solution.py:18
  116.8 11.0 %collective-permute-start.6 = (f32[2,10,10]{2,1,0:T(8,128)S(1)}, f32[2,10,10]{2,1,0:T(8,128)S(1)}, u32[]{:S(2)}, u32[]{:S(2)}) collective-permute-start(f32[2,10,10]{2,1,0:T(8,128)S(1)} %select_select_fusion.1), channel_id=1, source_target_pairs={{0,256},{256,0},{4,260},{260,4},{8,264},{264,8},{12,268},{268,12},... | collective-permute-start | bytes 2408 | tf_op jit(solution)/shard_map/ppermute | solution.py:18
where the time goes:
time: 135 us; the launch traced here: 134 us
  waiting for transfers between devices  43.8 us (32%)
  starting transfers between devices  38.4 us (28%)
  other arithmetic  26.3 us (19%)
  local copies, waits for them, and re-layouts  19 us (14%)
  matrix products  5.48 us (4%)
    ppermute x7, starting transfers between devices, partner_2(): return lax.ppermute(block, axis, route)  30.4 us
    all_to_all x1, waiting for transfers between devices, on_device(): lax.all_to_all(snapshots, 'tm', split_axis=2, concat_axis=0, tiled=True)  18.9 us
    ppermute x7, waiting for transfers between devices, partner_2(): return lax.ppermute(block, axis, route)  18.3 us
    another operation x22, other arithmetic, on_device(): lower = jnp.linalg.cholesky(outer_sum(lower, partner))  13.9 us
    unnamed x13, local copies, waits for them, and re-layouts  11.9 us
    all_to_all x1, waiting for transfers between devices, on_device(): lax.all_to_all(local_spec, 'tm', split_axis=0, concat_axis=2, tiled=True)  6.63 us
    all_to_all x1, other arithmetic, on_device(): lax.all_to_all(snapshots, 'tm', split_axis=2, concat_axis=0, tiled=True)  6.05 us
    all_to_all x1, starting transfers between devices, on_device(): lax.all_to_all(snapshots, 'tm', split_axis=2, concat_axis=0, tiled=True)  4.42 us
  transfers between devices with their start and end apart: 9, of which 9 were waited for; matrix products, arithmetic and copies ran while one was open for 1% of the time, Pallas kernels for 0%

commit v1 on v0

v1 whole, which is shorter than its diff:
```python
import functools

import jax
import jax.numpy as jnp
from jax import lax
from jax.experimental import pallas as pl
from jax.experimental.pallas import tpu as pltpu
from jax.sharding import PartitionSpec as P

NFFT = 128
NF = 8
NB = 5
COLS = 2 * NB
SLOTS = NB - 1
TWO_PI = 6.283185307179586


def pieces(x):
    high = x.astype(jnp.bfloat16)
    rest = x - high.astype(jnp.float32)
    middle = rest.astype(jnp.bfloat16)
    low = (rest - middle.astype(jnp.float32)).astype(jnp.bfloat16)
    return high, middle, low


def dot(a, b, contract=((1,), (0,))):
    return lax.dot_general(a, b, (contract, ((), ())), preferred_element_type=jnp.float32)


def transform_kernel(freq_ref, start_ref, x_ref, out_ref, table_ref):
    tdev = x_ref.shape[1]
    cells = x_ref.shape[2]

    @pl.when(pl.program_id(0) == 0)
    def _():
        quarter = lax.axis_index("tm")
        first = jnp.where(quarter >= 2, 1, 0)
        sub = lax.broadcasted_iota(jnp.int32, (8, tdev), 0)
        time = lax.broadcasted_iota(jnp.int32, (8, tdev), 1) + quarter * tdev
        slot = sub % SLOTS
        start = jnp.zeros((8, tdev), jnp.int32)
        for s in range(SLOTS):
            start = jnp.where(slot == s, start_ref[first + s], start)
        tau = time - start
        valid = (tau >= 0) & (tau < NFFT)
        hann = jnp.where(valid, 0.5 - 0.5 * jnp.cos(TWO_PI / NFFT * tau.astype(jnp.float32)), 0.0)
        turn = jnp.where(sub >= SLOTS, NFFT // 4, 0)
        rows = []
        for g in range(NF):
            phase = (freq_ref[g] * tau + turn) & (NFFT - 1)
            rows.append(hann * jnp.cos(TWO_PI / NFFT * phase.astype(jnp.float32)))
        table = jnp.concatenate(rows, axis=0)
        high, middle, low = pieces(table)
        table_ref[0] = high
        table_ref[1] = middle
        table_ref[2] = low

    a0, a1, a2 = table_ref[0], table_ref[1], table_ref[2]
    x0, x1, x2 = pieces(x_ref[0])
    total = dot(a0, x2) + dot(a2, x0) + dot(a1, x1)
    total = total + dot(a0, x1) + dot(a1, x0)
    total = total + dot(a0, x0)
    out_ref[...] = total.reshape(4, 2 * COLS - 4, cells)


def transform(snapshots, freq_index, block_start):
    tdev, nvar, cells = snapshots.shape
    x = jnp.transpose(snapshots, (1, 0, 2))
    return pl.pallas_call(
        transform_kernel,
        grid=(nvar,),
        out_shape=jax.ShapeDtypeStruct((4, 16, nvar * cells), jnp.float32),
        in_specs=[
            pl.BlockSpec(memory_space=pltpu.SMEM),
            pl.BlockSpec(memory_space=pltpu.SMEM),
            pl.BlockSpec((1, tdev, cells), lambda v: (v, 0, 0)),
        ],
        out_specs=pl.BlockSpec((4, 16, cells), lambda v: (0, 0, v)),
        scratch_shapes=[pltpu.VMEM((3, 64, tdev), jnp.bfloat16)],
        name="transform",
    )(freq_index, block_start, x)


def gram_kernel(parts_ref, vol_ref, stack_ref, packed_ref):
    width = parts_ref.shape[2]
    nvar = width // vol_ref.shape[1]
    root = jnp.sqrt(vol_ref[...])
    root = jnp.concatenate([root] * nvar, axis=1)
    sub = lax.broadcasted_iota(jnp.int32, (8, width), 0)
    tiles = []
    for f in range(2):
        rows = slice(8 * f, 8 * f + 8)
        early = parts_ref[0, rows, :] + parts_ref[1, rows, :]
        late = parts_ref[2, rows, :] + parts_ref[3, rows, :]
        early1 = pltpu.roll(early, 1, 0)
        late1 = pltpu.roll(late, 1, 0)
        late2 = pltpu.roll(late, 2, 0)
        upper = jnp.where(sub < 4, early, jnp.where(sub >= 5, early1, 0.0))
        upper = upper + jnp.where((sub >= 1) & (sub < 5), late1, jnp.where(sub >= 6, late2, 0.0))
        lower = jnp.where(sub < 1, early1, 0.0) + jnp.where(sub < 2, late2, 0.0)
        tiles += [upper * root, lower * root]
    weighted = jnp.concatenate(tiles, axis=0)
    stack = jnp.concatenate(pieces(weighted), axis=0)
    stack_ref[...] = stack
    full = dot(stack, stack, ((1,), (1,)))
    full = full[0:32] + full[32:64] + full[64:96]
    full = full[:, 0:32] + full[:, 32:64] + full[:, 64:96]
    full = jnp.concatenate([full, jnp.zeros((32, 96), jnp.float32)], axis=1)
    row = lax.broadcasted_iota(jnp.int32, (16, 128), 0)
    lane = lax.broadcasted_iota(jnp.int32, (16, 128), 1)
    both = jnp.where(lane <= row, full[0:16], pltpu.roll(full[16:32], 128 - 15, 1))
    both = jnp.where((row < COLS) & (lane <= COLS), both, 0.0)
    moved = jnp.zeros((8, 128), jnp.float32)
    for i in range(COLS):
        tile = both[0:8] if i < 8 else both[8:16]
        tile = jnp.where(row[0:8] == i % 8, tile, 0.0)
        moved = moved + (pltpu.roll(tile, i * (COLS + 1), 1) if i else tile)
    packed_ref[...] = jnp.broadcast_to(jnp.sum(moved, axis=0, keepdims=True), packed_ref.shape)


def modes_kernel(rows_total, gram_ref, stack_ref, modes_ref, triangle_ref, inverse_ref, upper_ref):
    nvar = modes_ref.shape[1]
    cells = modes_ref.shape[3]
    total = jnp.sum(gram_ref[...], axis=0, keepdims=True)
    row = lax.broadcasted_iota(jnp.int32, (16, 128), 0)
    lane = lax.broadcasted_iota(jnp.int32, (16, 128), 1)
    total = jnp.broadcast_to(total, (8, 128))
    spread = [jnp.zeros((8, 128), jnp.float32)] * 2
    for i in range(COLS):
        moved = pltpu.roll(total, 128 - i * (COLS + 1), 1) if i else total
        spread[i // 8] = jnp.where(row[0:8] == i % 8, moved, spread[i // 8])
    spread = jnp.concatenate(spread, axis=0)
    first = jnp.where((lane <= row) & (row < COLS), spread, 0.0)
    first = jnp.transpose(jnp.concatenate([first, jnp.zeros((112, 128), jnp.float32)], axis=0))[0:16]
    second = pltpu.roll(spread, 127, 1)
    second = jnp.where((lane >= row) & (lane < COLS), second, 0.0)
    eye = jnp.where(lane == row + 16, 1.0, 0.0)
    for f, a in enumerate((first, second)):
        a = a + eye
        pivots = jnp.ones((16, 128), jnp.float32)
        for k in range(COLS):
            pivot_row = jnp.broadcast_to(a[k : k + 1, :], (16, 128))
            pivot = jnp.broadcast_to(a[k : k + 1, k : k + 1], (16, 128))
            pivots = jnp.where(row == k, pivot, pivots)
            if k < COLS - 1:
                column = jnp.sum(jnp.where(lane == row, pivot_row, 0.0), axis=1, keepdims=True)
                factor = jnp.where(row > k, column / pivot, 0.0)
                a = a - factor * pivot_row
        scale = 1.0 / jnp.sqrt(pivots)
        a = a * scale
        inverse = jnp.where((lane >= 16) & (lane < 32), a, 0.0)
        inverse = inverse if f else pltpu.roll(inverse, 128 - 16, 1)
        inverse_ref[pl.ds(f, 16, stride=2), :] = inverse * jnp.sqrt(jnp.float32(rows_total))
        upper_ref[pl.ds(f, 16, stride=2), :] = jnp.where(lane >= row, a, 0.0)
    inverse = inverse_ref[...]
    inverse = inverse + pltpu.roll(inverse, 32, 1) + pltpu.roll(inverse, 64, 1)
    left = jnp.concatenate([x[:, 0:96] for x in pieces(inverse)], axis=0)
    tri = upper_ref[...] / jnp.sqrt(jnp.float32(rows_total * NFFT))
    for j in range(COLS):
        triangle_ref[j] = tri[2 * j : 2 * j + 2, 0:COLS]
    for v in range(nvar):
        x = dot(left, stack_ref[:, v * cells : (v + 1) * cells])
        x = x[64:96] + x[32:64] + x[0:32]
        for j in range(COLS):
            modes_ref[j, v] = x[2 * j : 2 * j + 2, :]


def on_device(snapshots, volumes, freq_index, block_start):
    tdev, nvar, cells = snapshots.shape
    cell_count = lax.axis_size("cell")
    width = nvar * cells
    parts = transform(snapshots, freq_index, block_start)
    parts = lax.all_to_all(parts, "tm", 0, 0, tiled=True)
    stack, packed = pl.pallas_call(
        gram_kernel,
        out_shape=(
            jax.ShapeDtypeStruct((96, width), jnp.bfloat16),
            jax.ShapeDtypeStruct((cell_count, 128), jnp.float32),
        ),
        name="gram",
    )(parts, volumes.reshape(1, cells))
    shares = lax.all_to_all(packed, "cell", 0, 0, tiled=True)
    modes, triangle = pl.pallas_call(
        functools.partial(modes_kernel, width * cell_count),
        out_shape=(
            jax.ShapeDtypeStruct((COLS, nvar, 2, cells), jnp.float32),
            jax.ShapeDtypeStruct((COLS, 2, COLS), jnp.float32),
        ),
        scratch_shapes=[pltpu.VMEM((32, 128), jnp.float32), pltpu.VMEM((32, 128), jnp.float32)],
        name="modes",
    )(shares, stack)
    return jnp.transpose(modes, (2, 0, 1, 3)), jnp.transpose(triangle, (1, 0, 2))


def solution(mesh):
    placed = (P("tm", None, "cell"), P("cell"), P(), P())
    return jax.shard_map(
        on_device,
        mesh=mesh,
        in_specs=placed,
        out_specs=(P("tm", None, None, "cell"), P("tm", None, None)),
        check_vma=False,
    )
```

time: 135 us -> 62.7 us (0.46)
  the two profiles are of different devices: /device:TPU:40 before, /device:TPU:1 now
where the time goes in v1:
time: 62.7 us; the launch traced here: 62.3 us
  blocking collectives  34.5 us (55%)
  Pallas kernels  11.9 us (19%)
  waiting for transfers between devices  8.81 us (14%)
  starting transfers between devices  4.97 us (8%)
  local copies, waits for them, and re-layouts  1.54 us (2%)
  between operations  0.64 us (1%)
    all_to_all x1, blocking collectives, on_device(): shares = lax.all_to_all(packed, 'cell', 0, 0, tiled=True)  34.5 us
    all_to_all x1, waiting for transfers between devices, on_device(): parts = lax.all_to_all(parts, 'tm', 0, 0, tiled=True)  8.81 us
    all_to_all x1, starting transfers between devices, on_device(): parts = lax.all_to_all(parts, 'tm', 0, 0, tiled=True)  4.97 us
    pallas_call x1, Pallas kernels, transform(): pl.pallas_call(transform_kernel, grid=(nvar,), out_shape=jax.ShapeDtypeSt...  4.88 us
    pallas_call x1, Pallas kernels, on_device(): pl.pallas_call(functools.partial(modes_kernel, width * cell_count), out_s...  4.54 us
    pallas_call x1, Pallas kernels, on_device(): pl.pallas_call(gram_kernel, out_shape=(jax.ShapeDtypeStruct((96, width),...  2.47 us
  transfers between devices with their start and end apart: 1, of which 1 were waited for; matrix products, arithmetic and copies ran while one was open for 1% of the time, Pallas kernels for 0%

profile of v1, /device:TPU:1, one launch (start us, length us, event | category | flops | bytes accessed | tf_op | source)
XLA Modules:
  0.0 62.3 jit_solution(4064809259430702910)
XLA Ops:
  0.6 4.9 %transform.1 = f32[4,16,3840]{2,1,0:T(8,128)} custom-call(s32[8]{0:T(128)} %freq_ref.1, s32[5]{0:T(128)} %start_ref.1, f32[5,96,768]{2,1,0:T(8,128)} %bitcast.7), custom_call_target="tpu_custom_call" | custom-call | tf_op jit(solution)/shard_map/transform/pallas_call | solution.py:69
  5.5 0.0 copy-start.1
  5.5 5.0 %all-to-all-start = ((f32[4,16,3840]{2,1,0:T(8,128)}), f32[4,16,3840]{2,1,0:T(8,128)S(1)}, u32[]{:S(2)}, u32[]{:S(2)}) async-start(f32[4,16,3840]{2,1,0:T(8,128)} %transform.1), calls=%async_computation | async-start | bytes 1966080 | tf_op jit(solution)/shard_map/all_to_all | solution.py:173
  10.5 0.0 copy-done.1
  10.5 0.6 reshape.9.vol_ref
  11.1 8.8 %all-to-all-done.parts_ref = f32[4,16,3840]{2,1,0:T(8,128)S(1)} async-done(((f32[4,16,3840]{2,1,0:T(8,128)}), f32[4,16,3840]{2,1,0:T(8,128)S(1)}, u32[]{:S(2)}, u32[]{:S(2)}) %all-to-all-start) | async-done | bytes 983072 | tf_op jit(solution)/shard_map/all_to_all | solution.py:173
  19.9 0.0 copy-start
  19.9 1.0 %copy-done = f32[4,16,3840]{2,1,0:T(8,128)} copy-done((f32[4,16,3840]{2,1,0:T(8,128)}, f32[4,16,3840]{2,1,0:T(8,128)S(1)}, u32[]{:S(2)}) %copy-start) | copy-done | bytes 983064
  20.8 2.5 %gram.1 = (bf16[96,3840]{1,0:T(8,128)(2,1)}, f32[128,128]{1,0:T(8,128)}) custom-call(f32[4,16,3840]{2,1,0:T(8,128)} %copy-done, f32[1,768]{1,0:T(1,128)} %reshape.9.vol_ref), custom_call_target="tpu_custom_call" | custom-call | tf_op jit(solution)/shard_map/gram/pallas_call | solution.py:174
  23.3 34.5 %all_to_all.16 = f32[128,1,128]{2,1,0:T(1,128)} all-to-all(f32[128,1,128]{2,1,0:T(1,128)} %bitcast.9), channel_id=1, replica_groups=mesh['cell'=128,'tm'=4] {'cell'}, dimensions={0} | all-to-all | bytes 131072 | tf_op jit(solution)/shard_map/all_to_all | solution.py:182
  57.8 4.5 %modes.1 = (f32[10,5,2,768]{3,2,1,0:T(2,128)}, f32[10,2,10]{2,1,0:T(2,128)}) custom-call(f32[128,128]{1,0:T(8,128)} %bitcast.8, bf16[96,3840]{1,0:T(8,128)(2,1)} %get-tuple-element.7.stack_ref), custom_call_target="tpu_custom_call" | custom-call | tf_op jit(solution)/shard_map/modes/pallas_call | solution.py:183
Async XLA Ops:
  5.5 5.0 %copy-start.1 = (f32[768]{0:T(1024)S(1)}, f32[768]{0:T(1024)}, u32[]{:S(2)}) copy-start(f32[768]{0:T(1024)} %param.5) | copy-start | bytes 9220
  5.5 14.4 %all-to-all-start = ((f32[4,16,3840]{2,1,0:T(8,128)}), f32[4,16,3840]{2,1,0:T(8,128)S(1)}, u32[]{:S(2)}, u32[]{:S(2)}) async-start(f32[4,16,3840]{2,1,0:T(8,128)} %transform.1), calls=%async_computation | async-start | bytes 1966080 | tf_op jit(solution)/shard_map/all_to_all | solution.py:173
  19.9 1.0 %copy-start = (f32[4,16,3840]{2,1,0:T(8,128)}, f32[4,16,3840]{2,1,0:T(8,128)S(1)}, u32[]{:S(2)}) copy-start(f32[4,16,3840]{2,1,0:T(8,128)S(1)} %all-to-all-done.parts_ref) | copy-start | bytes 2949124

commit v2 on v0

v2 whole, which is shorter than its diff:
```python
import functools

import jax
import jax.numpy as jnp
from jax import lax
from jax.experimental import pallas as pl
from jax.experimental.pallas import tpu as pltpu
from jax.sharding import PartitionSpec as P

NFFT = 128
NF = 8
NB = 5
COLS = 2 * NB
SLOTS = NB - 1
TWO_PI = 6.283185307179586


def pieces(x):
    high = x.astype(jnp.bfloat16)
    rest = x - high.astype(jnp.float32)
    middle = rest.astype(jnp.bfloat16)
    low = (rest - middle.astype(jnp.float32)).astype(jnp.bfloat16)
    return high, middle, low


def dot(a, b, contract=((1,), (0,))):
    return lax.dot_general(a, b, (contract, ((), ())), preferred_element_type=jnp.float32)


def transform_kernel(freq_ref, start_ref, x_hbm, out_hbm, x_ref, out_ref, table_ref, in_sem, out_sem):
    nvar, tdev, cells = x_hbm.shape
    for v in range(nvar):
        pltpu.make_async_copy(x_hbm.at[v], x_ref.at[v], in_sem.at[v]).start()
    quarter = lax.axis_index("tm")
    first = jnp.where(quarter >= 2, 1, 0)
    sub = lax.broadcasted_iota(jnp.int32, (8, tdev), 0)
    time = lax.broadcasted_iota(jnp.int32, (8, tdev), 1) + quarter * tdev
    slot = sub % SLOTS
    start = jnp.zeros((8, tdev), jnp.int32)
    for s in range(SLOTS):
        start = jnp.where(slot == s, start_ref[first + s], start)
    tau = time - start
    valid = (tau >= 0) & (tau < NFFT)
    hann = jnp.where(valid, 0.5 - 0.5 * jnp.cos(TWO_PI / NFFT * tau.astype(jnp.float32)), 0.0)
    turn = jnp.where(sub >= SLOTS, NFFT // 4, 0)
    rows = []
    for g in range(NF):
        phase = (freq_ref[g] * tau + turn) & (NFFT - 1)
        rows.append(hann * jnp.cos(TWO_PI / NFFT * phase.astype(jnp.float32)))
    high, middle, low = pieces(jnp.concatenate(rows, axis=0))
    table_ref[:, 0:tdev] = jnp.concatenate([high, middle, low], axis=0)
    table_ref[:, tdev : 2 * tdev] = jnp.concatenate([high, middle, jnp.zeros_like(low)], axis=0)
    for v in range(nvar):
        at = slice(v * cells, (v + 1) * cells)
        pltpu.make_async_copy(x_hbm.at[v], x_ref.at[v], in_sem.at[v]).wait()
        x0, x1, x2 = pieces(x_ref[v])
        last = dot(table_ref[0:64, 0:tdev], x2)
        total = dot(table_ref[...], jnp.concatenate([x0, x1], axis=0))
        total = total[0:64] + (total[64:128] + (total[128:192] + last))
        out_ref[:, :, at] = total.reshape(4, 16, cells)
        pltpu.make_async_copy(out_ref.at[:, :, at], out_hbm.at[:, :, at], out_sem.at[v]).start()
    for v in range(nvar):
        at = slice(v * cells, (v + 1) * cells)
        pltpu.make_async_copy(out_ref.at[:, :, at], out_hbm.at[:, :, at], out_sem.at[v]).wait()


def transform(snapshots, freq_index, block_start):
    tdev, nvar, cells = snapshots.shape
    x = jnp.transpose(snapshots, (1, 0, 2))
    return pl.pallas_call(
        transform_kernel,
        out_shape=jax.ShapeDtypeStruct((4, 16, nvar * cells), jnp.float32),
        in_specs=[
            pl.BlockSpec(memory_space=pltpu.SMEM),
            pl.BlockSpec(memory_space=pltpu.SMEM),
            pl.BlockSpec(memory_space=pl.ANY),
        ],
        out_specs=pl.BlockSpec(memory_space=pl.ANY),
        scratch_shapes=[
            pltpu.VMEM((nvar, tdev, cells), jnp.float32),
            pltpu.VMEM((4, 16, nvar * cells), jnp.float32),
            pltpu.VMEM((192, 2 * tdev), jnp.bfloat16),
            pltpu.SemaphoreType.DMA((nvar,)),
            pltpu.SemaphoreType.DMA((nvar,)),
        ],
        name="transform",
    )(freq_index, block_start, x)


def gram_kernel(parts_ref, vol_ref, stack_ref, packed_ref):
    cells = vol_ref.shape[1]
    root = jnp.broadcast_to(jnp.sqrt(vol_ref[...]), (8, cells))
    sub = lax.broadcasted_iota(jnp.int32, (8, cells), 0)
    full = jnp.zeros((96, 96), jnp.float32)
    for v in range(parts_ref.shape[2] // cells):
        at = slice(v * cells, (v + 1) * cells)
        tiles = []
        for f in range(2):
            rows = slice(8 * f, 8 * f + 8)
            early = parts_ref[0, rows, at] + parts_ref[1, rows, at]
            late = parts_ref[2, rows, at] + parts_ref[3, rows, at]
            early1 = pltpu.roll(early, 1, 0)
            late1 = pltpu.roll(late, 1, 0)
            late2 = pltpu.roll(late, 2, 0)
            upper = jnp.where(sub < 4, early, jnp.where(sub >= 5, early1, 0.0))
            upper = upper + jnp.where((sub >= 1) & (sub < 5), late1, jnp.where(sub >= 6, late2, 0.0))
            lower = jnp.where(sub < 1, early1, 0.0) + jnp.where(sub < 2, late2, 0.0)
            tiles += [upper * root, lower * root]
        stack = jnp.concatenate(pieces(jnp.concatenate(tiles, axis=0)), axis=0)
        stack_ref[:, at] = stack
        full = full + dot(stack, stack, ((1,), (1,)))
    full = full[0:32] + full[32:64] + full[64:96]
    full = full[:, 0:32] + full[:, 32:64] + full[:, 64:96]
    full = jnp.concatenate([full, jnp.zeros((32, 96), jnp.float32)], axis=1)
    row = lax.broadcasted_iota(jnp.int32, (8, 128), 0)
    lane = lax.broadcasted_iota(jnp.int32, (8, 128), 1)
    moved = jnp.zeros((8, 128), jnp.float32)
    for f in range(2):
        for i in range(COLS):
            at = 16 * f + i // 8 * 8
            tile = jnp.where((row == i % 8) & (lane >= 16 * f) & (lane <= 16 * f + i), full[at : at + 8], 0.0)
            shift = 48 * f + i * (i + 1) // 2
            moved = moved + (pltpu.roll(tile, shift, 1) if shift else tile)
    packed_ref[...] = jnp.broadcast_to(jnp.sum(moved, axis=0, keepdims=True), packed_ref.shape)


def gram(parts, volumes, cell_count):
    width = parts.shape[2]
    return pl.pallas_call(
        gram_kernel,
        out_shape=(
            jax.ShapeDtypeStruct((96, width), jnp.bfloat16),
            jax.ShapeDtypeStruct((cell_count, 128), jnp.float32),
        ),
        compiler_params=pltpu.CompilerParams(vmem_limit_bytes=12 << 20),
        name="gram",
    )(parts, volumes.reshape(1, volumes.shape[0]))


def modes_kernel(rows_total, gram_ref, stack_ref, modes_hbm, triangle_ref, modes_ref, entry_ref, left_ref, sem):
    nvar = modes_ref.shape[1]
    cells = modes_ref.shape[3]
    total = jnp.broadcast_to(jnp.sum(gram_ref[...], axis=0, keepdims=True), (128, 128))
    total = jnp.transpose(total)
    entry_ref[...] = jnp.where(lax.broadcasted_iota(jnp.int32, (64, 128), 1) < 64, total[0:64], total[64:128])
    a = {}
    for i in range(COLS):
        for j in range(i + 1):
            a[i, j] = jnp.broadcast_to(entry_ref[pl.ds(i * (i + 1) // 2 + j, 1), :], (8, 128))
    low = {}
    for k in range(COLS):
        inverse = 1.0 / a[k, k]
        for i in range(k + 1, COLS):
            low[i, k] = a[i, k] * inverse
        for i in range(k + 1, COLS):
            for j in range(k + 1, i + 1):
                a[i, j] = a[i, j] - low[i, k] * a[j, k]
    lane = lax.broadcasted_iota(jnp.int32, (8, 128), 1) & 63
    rows = jnp.sqrt(jnp.float32(rows_total))
    shrink = 1.0 / jnp.sqrt(jnp.float32(rows_total * NFFT))
    turned = {}
    for i in range(COLS):
        scale = 1.0 / jnp.sqrt(a[i, i])
        left = jnp.where(lane == i, 1.0, 0.0)
        for j in range(i):
            x = low[i, j]
            for k in range(j + 1, i):
                x = x + low[i, k] * turned[k, j]
            turned[i, j] = -x
            left = jnp.where(lane == j, turned[i, j], left)
        left_ref[2 * i : 2 * i + 2, :] = (left * (scale * rows))[0:2]
        upper = jnp.zeros((8, 128), jnp.float32)
        for k in range(i, COLS):
            upper = jnp.where(lane == k, a[k, i], upper)
        upper = upper * (scale * shrink)
        triangle_ref[i] = jnp.where(
            lax.broadcasted_iota(jnp.int32, (8, 128), 0) == 0, upper, pltpu.roll(upper, 64, 1)
        )[0:2, 0:COLS]
    lane = lax.broadcasted_iota(jnp.int32, (32, 128), 1)
    row = lax.broadcasted_iota(jnp.int32, (32, 128), 0)
    left = left_ref[...]
    left = jnp.where((row & 1) == 0, jnp.where(lane < 16, left, 0.0), jnp.where((lane >= 16) & (lane < 32), pltpu.roll(left, 80, 1), 0.0))
    left = jnp.where(row < 2 * COLS, left, 0.0)
    left = left + pltpu.roll(left, 32, 1) + pltpu.roll(left, 64, 1)
    left = jnp.concatenate([x[:, 0:96] for x in pieces(left)], axis=0)
    copies = []
    for v in range(nvar):
        x = dot(left, stack_ref[:, v * cells : (v + 1) * cells])
        x = x[64:96] + x[32:64] + x[0:32]
        for j in range(COLS):
            modes_ref[j, v] = x[2 * j : 2 * j + 2, :]
        copies.append(pltpu.make_async_copy(modes_ref.at[:, v], modes_hbm.at[:, v], sem.at[v]))
        copies[-1].start()
    for copy in copies:
        copy.wait()


def modes_of(shares, stack, nvar, cells, cell_count):
    return pl.pallas_call(
        functools.partial(modes_kernel, nvar * cells * cell_count),
        out_shape=(
            jax.ShapeDtypeStruct((COLS, nvar, 2, cells), jnp.float32),
            jax.ShapeDtypeStruct((COLS, 2, COLS), jnp.float32),
        ),
        out_specs=(pl.BlockSpec(memory_space=pl.ANY), pl.BlockSpec(memory_space=pltpu.VMEM)),
        scratch_shapes=[
            pltpu.VMEM((COLS, nvar, 2, cells), jnp.float32),
            pltpu.VMEM((64, 128), jnp.float32),
            pltpu.VMEM((32, 128), jnp.float32),
            pltpu.SemaphoreType.DMA((nvar,)),
        ],
        compiler_params=pltpu.CompilerParams(vmem_limit_bytes=12 << 20),
        name="modes",
    )(shares, stack)


def chain(snapshots, volumes, freq_index, block_start, exchange, share, cell_count):
    tdev, nvar, cells = snapshots.shape
    parts = exchange(transform(snapshots, freq_index, block_start))
    stack, packed = gram(parts, volumes, cell_count)
    modes, triangle = modes_of(share(packed), stack, nvar, cells, cell_count)
    return jnp.transpose(modes, (2, 0, 1, 3)), jnp.transpose(triangle, (1, 0, 2))


def on_device(snapshots, volumes, freq_index, block_start):
    return chain(
        snapshots,
        volumes,
        freq_index,
        block_start,
        lambda x: lax.all_to_all(x, "tm", 0, 0, tiled=True),
        lambda x: lax.all_to_all(x, "cell", 0, 0, tiled=True),
        lax.axis_size("cell"),
    )


def solution(mesh):
    placed = (P("tm", None, "cell"), P("cell"), P(), P())
    return jax.shard_map(
        on_device,
        mesh=mesh,
        in_specs=placed,
        out_specs=(P("tm", None, None, "cell"), P("tm", None, None)),
        check_vma=False,
    )
```

time: 135 us -> 56 us (0.41)
  the two profiles are of different devices: /device:TPU:40 before, /device:TPU:1 now
where the time goes in v2:
time: 56 us; the launch traced here: 55.8 us
  blocking collectives  34.2 us (61%)
  waiting for transfers between devices  9.38 us (17%)
  Pallas kernels  6.71 us (12%)
  starting transfers between devices  4.84 us (9%)
  between operations  0.66 us (1%)
    all_to_all x1, blocking collectives, on_device(): lax.all_to_all(x, 'cell', 0, 0, tiled=True)  34.2 us
    all_to_all x1, waiting for transfers between devices, on_device(): lax.all_to_all(x, 'tm', 0, 0, tiled=True)  9.38 us
    all_to_all x1, starting transfers between devices, on_device(): lax.all_to_all(x, 'tm', 0, 0, tiled=True)  4.84 us
    pallas_call x1, Pallas kernels, transform(): pl.pallas_call(transform_kernel, out_shape=jax.ShapeDtypeStruct((4, 16, n...  4.12 us
    pallas_call x1, Pallas kernels, modes_of(): pl.pallas_call(functools.partial(modes_kernel, nvar * cells * cell_count)...  1.99 us
  transfers between devices with their start and end apart: 1, of which 1 were waited for; matrix products, arithmetic and copies ran while one was open for 0% of the time, Pallas kernels for 0%

profile of v2, /device:TPU:1, one launch (start us, length us, event | category | flops | bytes accessed | tf_op | source)
XLA Modules:
  0.0 55.8 jit_solution(6578504654003912380)
XLA Ops:
  0.6 4.1 %transform.1 = f32[4,16,3840]{2,1,0:T(8,128)} custom-call(s32[8]{0:T(128)} %freq_ref.1, s32[5]{0:T(128)} %start_ref.1, f32[5,96,768]{2,1,0:T(8,128)} %bitcast.9), custom_call_target="tpu_custom_call" | custom-call | tf_op jit(solution)/shard_map/transform/pallas_call | solution.py:70
  4.8 0.0 copy-start
  4.8 4.8 %all-to-all-start = ((f32[4,16,3840]{2,1,0:T(8,128)}), f32[4,16,3840]{2,1,0:T(8,128)S(1)}, u32[]{:S(2)}, u32[]{:S(2)}) async-start(f32[4,16,3840]{2,1,0:T(8,128)} %transform.1), calls=%async_computation | async-start | bytes 1966080 | tf_op jit(solution)/shard_map/all_to_all | solution.py:231
  9.6 0.0 copy-done
  9.6 9.4 %all-to-all-done.parts_ref = f32[4,16,3840]{2,1,0:T(8,128)S(1)} async-done(((f32[4,16,3840]{2,1,0:T(8,128)}), f32[4,16,3840]{2,1,0:T(8,128)S(1)}, u32[]{:S(2)}, u32[]{:S(2)}) %all-to-all-start) | async-done | bytes 983072 | tf_op jit(solution)/shard_map/all_to_all | solution.py:231
  19.0 0.6 %gram.1 = (bf16[96,3840]{1,0:T(8,128)(2,1)S(1)}, f32[128,128]{1,0:T(8,128)S(1)}) custom-call(f32[4,16,3840]{2,1,0:T(8,128)S(1)} %all-to-all-done.parts_ref, f32[1,768]{1,0:T(1,128)S(1)} %reshape.9.vol_ref), custom_call_target="tpu_custom_call" | custom-call | tf_op jit(solution)/shard_map/gram/pallas_call | solution.py:129
  19.6 34.2 %all_to_all.16 = f32[128,1,128]{2,1,0:T(1,128)S(1)} all-to-all(f32[128,1,128]{2,1,0:T(1,128)S(1)} %bitcast.8), channel_id=1, replica_groups=mesh['cell'=128,'tm'=4] {'cell'}, dimensions={0} | all-to-all | bytes 131072 | tf_op jit(solution)/shard_map/all_to_all | solution.py:232
  53.8 2.0 %modes.1 = (f32[10,5,2,768]{3,2,1,0:T(2,128)}, f32[10,2,10]{2,1,0:T(2,128)}) custom-call(f32[128,128]{1,0:T(8,128)S(1)} %bitcast.7, bf16[96,3840]{1,0:T(8,128)(2,1)S(1)} %get-tuple-element.7.stack_ref), custom_call_target="tpu_custom_call" | custom-call | tf_op jit(solution)/shard_map/modes/pallas_call | solution.py:199
  (1 shorter events, 0.0 us)
Async XLA Ops:
  4.8 4.9 %copy-start = (f32[768]{0:T(1024)S(1)}, f32[768]{0:T(1024)}, u32[]{:S(2)}) copy-start(f32[768]{0:T(1024)} %param.5) | copy-start | bytes 9220
  4.8 14.2 %all-to-all-start = ((f32[4,16,3840]{2,1,0:T(8,128)}), f32[4,16,3840]{2,1,0:T(8,128)S(1)}, u32[]{:S(2)}, u32[]{:S(2)}) async-start(f32[4,16,3840]{2,1,0:T(8,128)} %transform.1), calls=%async_computation | async-start | bytes 1966080 | tf_op jit(solution)/shard_map/all_to_all | solution.py:231

commit v3 on v2

--- a/solution.py
+++ b/solution.py
@@ -27,8 +27,17 @@
     return lax.dot_general(a, b, (contract, ((), ())), preferred_element_type=jnp.float32)
 
 
-def transform_kernel(freq_ref, start_ref, x_hbm, out_hbm, x_ref, out_ref, table_ref, in_sem, out_sem):
+def transform_kernel(
+    freq_hbm, start_hbm, vol_hbm, x_hbm, out_ref, freq_ref, start_ref, vol_ref, x_ref, table_ref, small_sem, in_sem
+):
     nvar, tdev, cells = x_hbm.shape
+    small = [
+        pltpu.make_async_copy(freq_hbm, freq_ref, small_sem.at[0]),
+        pltpu.make_async_copy(start_hbm, start_ref, small_sem.at[1]),
+        pltpu.make_async_copy(vol_hbm, vol_ref, small_sem.at[2]),
+    ]
+    for copy in small:
+        copy.start()
     for v in range(nvar):
         pltpu.make_async_copy(x_hbm.at[v], x_ref.at[v], in_sem.at[v]).start()
     quarter = lax.axis_index("tm")
@@ -36,6 +45,8 @@
     sub = lax.broadcasted_iota(jnp.int32, (8, tdev), 0)
     time = lax.broadcasted_iota(jnp.int32, (8, tdev), 1) + quarter * tdev
     slot = sub % SLOTS
+    for copy in small:
+        copy.wait()
     start = jnp.zeros((8, tdev), jnp.int32)
     for s in range(SLOTS):
         start = jnp.where(slot == s, start_ref[first + s], start)
@@ -50,6 +61,7 @@
     high, middle, low = pieces(jnp.concatenate(rows, axis=0))
     table_ref[:, 0:tdev] = jnp.concatenate([high, middle, low], axis=0)
     table_ref[:, tdev : 2 * tdev] = jnp.concatenate([high, middle, jnp.zeros_like(low)], axis=0)
+    root = jnp.sqrt(vol_ref[...]).reshape(1, cells)
     for v in range(nvar):
         at = slice(v * cells, (v + 1) * cells)
         pltpu.make_async_copy(x_hbm.at[v], x_ref.at[v], in_sem.at[v]).wait()
@@ -57,39 +69,32 @@
         last = dot(table_ref[0:64, 0:tdev], x2)
         total = dot(table_ref[...], jnp.concatenate([x0, x1], axis=0))
         total = total[0:64] + (total[64:128] + (total[128:192] + last))
-        out_ref[:, :, at] = total.reshape(4, 16, cells)
-        pltpu.make_async_copy(out_ref.at[:, :, at], out_hbm.at[:, :, at], out_sem.at[v]).start()
-    for v in range(nvar):
-        at = slice(v * cells, (v + 1) * cells)
-        pltpu.make_async_copy(out_ref.at[:, :, at], out_hbm.at[:, :, at], out_sem.at[v]).wait()
-
-
-def transform(snapshots, freq_index, block_start):
+        out_ref[:, :, at] = (total * root).reshape(4, 16, cells)
+
+
+def transform(snapshots, volumes, freq_index, block_start):
     tdev, nvar, cells = snapshots.shape
     x = jnp.transpose(snapshots, (1, 0, 2))
     return pl.pallas_call(
         transform_kernel,
         out_shape=jax.ShapeDtypeStruct((4, 16, nvar * cells), jnp.float32),
-        in_specs=[
-            pl.BlockSpec(memory_space=pltpu.SMEM),
-            pl.BlockSpec(memory_space=pltpu.SMEM),
-            pl.BlockSpec(memory_space=pl.ANY),
-        ],
-        out_specs=pl.BlockSpec(memory_space=pl.ANY),
+        in_specs=[pl.BlockSpec(memory_space=pltpu.HBM)] * 4,
+        out_specs=pl.BlockSpec(memory_space=pltpu.VMEM),
         scratch_shapes=[
+            pltpu.SMEM((NF,), jnp.int32),
+            pltpu.SMEM((NB,), jnp.int32),
+            pltpu.VMEM((cells,), jnp.float32),
             pltpu.VMEM((nvar, tdev, cells), jnp.float32),
-            pltpu.VMEM((4, 16, nvar * cells), jnp.float32),
             pltpu.VMEM((192, 2 * tdev), jnp.bfloat16),
-            pltpu.SemaphoreType.DMA((nvar,)),
+            pltpu.SemaphoreType.DMA((3,)),
             pltpu.SemaphoreType.DMA((nvar,)),
         ],
+        compiler_params=pltpu.CompilerParams(vmem_limit_bytes=8 << 20),
         name="transform",
-    )(freq_index, block_start, x)
-
-
-def gram_kernel(parts_ref, vol_ref, stack_ref, packed_ref):
-    cells = vol_ref.shape[1]
-    root = jnp.broadcast_to(jnp.sqrt(vol_ref[...]), (8, cells))
+    )(*(pltpu.with_memory_space_constraint(a, pltpu.HBM) for a in (freq_index, block_start, volumes, x)))
+
+
+def gram_kernel(cells, parts_ref, stack_ref, packed_ref):
     sub = lax.broadcasted_iota(jnp.int32, (8, cells), 0)
     full = jnp.zeros((96, 96), jnp.float32)
     for v in range(parts_ref.shape[2] // cells):
@@ -105,7 +110,7 @@
             upper = jnp.where(sub < 4, early, jnp.where(sub >= 5, early1, 0.0))
             upper = upper + jnp.where((sub >= 1) & (sub < 5), late1, jnp.where(sub >= 6, late2, 0.0))
             lower = jnp.where(sub < 1, early1, 0.0) + jnp.where(sub < 2, late2, 0.0)
-            tiles += [upper * root, lower * root]
+            tiles += [upper, lower]
         stack = jnp.concatenate(pieces(jnp.concatenate(tiles, axis=0)), axis=0)
         stack_ref[:, at] = stack
         full = full + dot(stack, stack, ((1,), (1,)))
@@ -124,17 +129,17 @@
     packed_ref[...] = jnp.broadcast_to(jnp.sum(moved, axis=0, keepdims=True), packed_ref.shape)
 
 
-def gram(parts, volumes, cell_count):
+def gram(parts, cells, cell_count):
     width = parts.shape[2]
     return pl.pallas_call(
-        gram_kernel,
+        functools.partial(gram_kernel, cells),
         out_shape=(
             jax.ShapeDtypeStruct((96, width), jnp.bfloat16),
             jax.ShapeDtypeStruct((cell_count, 128), jnp.float32),
         ),
         compiler_params=pltpu.CompilerParams(vmem_limit_bytes=12 << 20),
         name="gram",
-    )(parts, volumes.reshape(1, volumes.shape[0]))
+    )(parts)
 
 
 def modes_kernel(rows_total, gram_ref, stack_ref, modes_hbm, triangle_ref, modes_ref, entry_ref, left_ref, sem):
@@ -216,8 +221,8 @@
 
 def chain(snapshots, volumes, freq_index, block_start, exchange, share, cell_count):
     tdev, nvar, cells = snapshots.shape
-    parts = exchange(transform(snapshots, freq_index, block_start))
-    stack, packed = gram(parts, volumes, cell_count)
+    parts = exchange(transform(snapshots, volumes, freq_index, block_start))
+    stack, packed = gram(parts, cells, cell_count)
     modes, triangle = modes_of(share(packed), stack, nvar, cells, cell_count)
     return jnp.transpose(modes, (2, 0, 1, 3)), jnp.transpose(triangle, (1, 0, 2))
 

time: 56 us -> 54.6 us (0.975)
  blocking collectives: 34.2 us -> 48.2 us
  waiting for transfers between devices: 9.38 us -> 0 us
  starting transfers between devices: 4.84 us -> 0 us
  Pallas kernels: 6.71 us -> 5.62 us
    all_to_all x0 -> x1, blocking collectives: none -> 14.2 us  [on_device(): lax.all_to_all(x, 'tm', 0, 0, tiled=True)]
    all_to_all x1 -> x0, waiting for transfers between devices: 9.38 us -> none  [on_device(): lax.all_to_all(x, 'tm', 0, 0, tiled=True)]
    all_to_all x1 -> x0, starting transfers between devices: 4.84 us -> none  [on_device(): lax.all_to_all(x, 'tm', 0, 0, tiled=True)]
    pallas_call x1, Pallas kernels: 4.12 us -> 3.05 us  [transform(): pl.pallas_call(transform_kernel, out_shape=jax.ShapeDtypeStruct((4, 16, n...]
  transfers between devices with their start and end apart: 1 -> 0, of which waited for: 1 -> 0; matrix products, arithmetic and copies ran while one was open for 0% -> 0% of each run, Pallas kernels for 0% -> 0%
where the time goes in v3:
time: 54.6 us; the launch traced here: 54.4 us
  blocking collectives  48.2 us (88%)
  Pallas kernels  5.62 us (10%)
  between operations  0.65 us (1%)
    all_to_all x1, blocking collectives, on_device(): lax.all_to_all(x, 'cell', 0, 0, tiled=True)  33.9 us
    all_to_all x1, blocking collectives, on_device(): lax.all_to_all(x, 'tm', 0, 0, tiled=True)  14.2 us
    pallas_call x1, Pallas kernels, transform(): pl.pallas_call(transform_kernel, out_shape=jax.ShapeDtypeStruct((4, 16, n...  3.05 us
    pallas_call x1, Pallas kernels, modes_of(): pl.pallas_call(functools.partial(modes_kernel, nvar * cells * cell_count)...  1.99 us

profile of v3, /device:TPU:1, one launch (start us, length us, event | category | flops | bytes accessed | tf_op | source)
XLA Modules:
  0.0 54.4 jit_solution(14499419637155338732)
XLA Ops:
  0.6 3.1 %transform.1 = f32[4,16,3840]{2,1,0:T(8,128)S(1)} custom-call(s32[8]{0:T(128)} %freq_hbm.1, s32[5]{0:T(128)} %start_hbm.1, f32[768]{0:T(1024)} %vol_hbm.1, f32[5,96,768]{2,1,0:T(8,128)} %bitcast.9), custom_call_target="tpu_custom_call" | custom-call | tf_op jit(solution)/shard_map/transform/pallas_call | solution.py:78
  3.7 14.2 %all_to_all.16.parts_ref = f32[4,16,3840]{2,1,0:T(8,128)S(1)} all-to-all(f32[4,16,3840]{2,1,0:T(8,128)S(1)} %transform.1), channel_id=1, replica_groups=mesh['cell'=128,'tm'=4] {'tm'}, dimensions={0} | all-to-all | bytes 1966080 | tf_op jit(solution)/shard_map/all_to_all | solution.py:236
  17.9 0.6 %gram.1 = (bf16[96,3840]{1,0:T(8,128)(2,1)S(1)}, f32[128,128]{1,0:T(8,128)S(1)}) custom-call(f32[4,16,3840]{2,1,0:T(8,128)S(1)} %all_to_all.16.parts_ref), custom_call_target="tpu_custom_call" | custom-call | tf_op jit(solution)/shard_map/gram/pallas_call | solution.py:134
  18.5 33.9 %all_to_all.17 = f32[128,1,128]{2,1,0:T(1,128)S(1)} all-to-all(f32[128,1,128]{2,1,0:T(1,128)S(1)} %bitcast.8), channel_id=1, replica_groups=mesh['cell'=128,'tm'=4] {'cell'}, dimensions={0} | all-to-all | bytes 131072 | tf_op jit(solution)/shard_map/all_to_all | solution.py:237
  52.4 2.0 %modes.1 = (f32[10,5,2,768]{3,2,1,0:T(2,128)}, f32[10,2,10]{2,1,0:T(2,128)}) custom-call(f32[128,128]{1,0:T(8,128)S(1)} %bitcast.7, bf16[96,3840]{1,0:T(8,128)(2,1)S(1)} %get-tuple-element.7.stack_ref), custom_call_target="tpu_custom_call" | custom-call | tf_op jit(solution)/shard_map/modes/pallas_call | solution.py:204

commit v4 on v3

--- a/solution.py
+++ b/solution.py
@@ -28,9 +28,13 @@
 
 
 def transform_kernel(
-    freq_hbm, start_hbm, vol_hbm, x_hbm, out_ref, freq_ref, start_ref, vol_ref, x_ref, table_ref, small_sem, in_sem
+    freq_hbm, start_hbm, vol_hbm, x_hbm, out_ref, freq_ref, start_ref, vol_ref, x_ref, piece_ref, table_ref, small_sem, in_sem
 ):
     nvar, tdev, cells = x_hbm.shape
+
+    def incoming(v):
+        return pltpu.make_async_copy(x_hbm.at[v], x_ref.at[v], in_sem.at[v])
+
     small = [
         pltpu.make_async_copy(freq_hbm, freq_ref, small_sem.at[0]),
         pltpu.make_async_copy(start_hbm, start_ref, small_sem.at[1]),
@@ -39,7 +43,7 @@
     for copy in small:
         copy.start()
     for v in range(nvar):
-        pltpu.make_async_copy(x_hbm.at[v], x_ref.at[v], in_sem.at[v]).start()
+        incoming(v).start()
     quarter = lax.axis_index("tm")
     first = jnp.where(quarter >= 2, 1, 0)
     sub = lax.broadcasted_iota(jnp.int32, (8, tdev), 0)
@@ -60,16 +64,34 @@
         rows.append(hann * jnp.cos(TWO_PI / NFFT * phase.astype(jnp.float32)))
     high, middle, low = pieces(jnp.concatenate(rows, axis=0))
     table_ref[:, 0:tdev] = jnp.concatenate([high, middle, low], axis=0)
-    table_ref[:, tdev : 2 * tdev] = jnp.concatenate([high, middle, jnp.zeros_like(low)], axis=0)
+    table_ref[:, tdev : 2 * tdev] = jnp.concatenate([high, middle, high], axis=0)
     root = jnp.sqrt(vol_ref[...]).reshape(1, cells)
-    for v in range(nvar):
-        at = slice(v * cells, (v + 1) * cells)
-        pltpu.make_async_copy(x_hbm.at[v], x_ref.at[v], in_sem.at[v]).wait()
-        x0, x1, x2 = pieces(x_ref[v])
-        last = dot(table_ref[0:64, 0:tdev], x2)
-        total = dot(table_ref[...], jnp.concatenate([x0, x1], axis=0))
-        total = total[0:64] + (total[64:128] + (total[128:192] + last))
-        out_ref[:, :, at] = (total * root).reshape(4, 16, cells)
+
+    def split(v, low):
+        rows = slice(low, low + 16)
+        x0, x1, x2 = pieces(x_ref[v, rows, :])
+        piece_ref[v, low : low + 16, :] = x1
+        piece_ref[v, tdev + low : tdev + low + 16, :] = x0
+        piece_ref[v, 2 * tdev + low : 2 * tdev + low + 16, :] = x2
+
+    def products(v, low):
+        lanes = slice(low, low + 256)
+        part = dot(table_ref[128:192], piece_ref[v, tdev : 3 * tdev, lanes])
+        total = dot(table_ref[0:128], piece_ref[v, 0 : 2 * tdev, lanes])
+        total = (total[0:64] + (total[64:128] + part)) * root[:, lanes]
+        out_ref[:, :, v * cells + low : v * cells + low + 256] = total.reshape(4, 16, 256)
+
+    blocks = tdev // 16
+    tiles = cells // 256
+    for v in range(nvar + 1):
+        if v < nvar:
+            incoming(v).wait()
+        for n in range(tiles):
+            if v < nvar:
+                for r in range(n * blocks // tiles, (n + 1) * blocks // tiles):
+                    split(v, 16 * r)
+            if v > 0:
+                products(v - 1, 256 * n)
 
 
 def transform(snapshots, volumes, freq_index, block_start):
@@ -85,6 +107,7 @@
             pltpu.SMEM((NB,), jnp.int32),
             pltpu.VMEM((cells,), jnp.float32),
             pltpu.VMEM((nvar, tdev, cells), jnp.float32),
+            pltpu.VMEM((nvar, 3 * tdev, cells), jnp.bfloat16),
             pltpu.VMEM((192, 2 * tdev), jnp.bfloat16),
             pltpu.SemaphoreType.DMA((3,)),
             pltpu.SemaphoreType.DMA((nvar,)),
@@ -142,7 +165,7 @@
     )(parts)
 
 
-def modes_kernel(rows_total, gram_ref, stack_ref, modes_hbm, triangle_ref, modes_ref, entry_ref, left_ref, sem):
+def modes_kernel(rows_total, gram_ref, stack_ref, modes_hbm, triangle_hbm, modes_ref, triangle_ref, entry_ref, left_ref, sem):
     nvar = modes_ref.shape[1]
     cells = modes_ref.shape[3]
     total = jnp.broadcast_to(jnp.sum(gram_ref[...], axis=0, keepdims=True), (128, 128))
@@ -188,7 +211,8 @@
     left = jnp.where(row < 2 * COLS, left, 0.0)
     left = left + pltpu.roll(left, 32, 1) + pltpu.roll(left, 64, 1)
     left = jnp.concatenate([x[:, 0:96] for x in pieces(left)], axis=0)
-    copies = []
+    copies = [pltpu.make_async_copy(triangle_ref, triangle_hbm, sem.at[nvar])]
+    copies[0].start()
     for v in range(nvar):
         x = dot(left, stack_ref[:, v * cells : (v + 1) * cells])
         x = x[64:96] + x[32:64] + x[0:32]
@@ -207,12 +231,13 @@
             jax.ShapeDtypeStruct((COLS, nvar, 2, cells), jnp.float32),
             jax.ShapeDtypeStruct((COLS, 2, COLS), jnp.float32),
         ),
-        out_specs=(pl.BlockSpec(memory_space=pl.ANY), pl.BlockSpec(memory_space=pltpu.VMEM)),
+        out_specs=(pl.BlockSpec(memory_space=pltpu.HBM), pl.BlockSpec(memory_space=pltpu.HBM)),
         scratch_shapes=[
             pltpu.VMEM((COLS, nvar, 2, cells), jnp.float32),
+            pltpu.VMEM((COLS, 2, COLS), jnp.float32),
             pltpu.VMEM((64, 128), jnp.float32),
             pltpu.VMEM((32, 128), jnp.float32),
-            pltpu.SemaphoreType.DMA((nvar,)),
+            pltpu.SemaphoreType.DMA((nvar + 1,)),
         ],
         compiler_params=pltpu.CompilerParams(vmem_limit_bytes=12 << 20),
         name="modes",

time: 54.6 us -> 53.6 us (0.982)
  Pallas kernels: 5.62 us -> 4.57 us
    pallas_call x1, Pallas kernels: 1.99 us -> 1.4 us  [modes_of(): pl.pallas_call(functools.partial(modes_kernel, nvar * cells * cell_count)...]
where the time goes in v4:
time: 53.6 us; the launch traced here: 53.4 us
  blocking collectives  48.2 us (90%)
  Pallas kernels  4.57 us (9%)
  between operations  0.65 us (1%)
    all_to_all x1, blocking collectives, on_device(): lax.all_to_all(x, 'cell', 0, 0, tiled=True)  34 us
    all_to_all x1, blocking collectives, on_device(): lax.all_to_all(x, 'tm', 0, 0, tiled=True)  14.2 us
    pallas_call x1, Pallas kernels, transform(): pl.pallas_call(transform_kernel, out_shape=jax.ShapeDtypeStruct((4, 16, n...  2.63 us
    pallas_call x1, Pallas kernels, modes_of(): pl.pallas_call(functools.partial(modes_kernel, nvar * cells * cell_count)...  1.4 us

profile of v4, /device:TPU:1, one launch (start us, length us, event | category | flops | bytes accessed | tf_op | source)
XLA Modules:
  0.0 53.4 jit_solution(14362517142731303617)
XLA Ops:
  0.6 2.6 %transform.1 = f32[4,16,3840]{2,1,0:T(8,128)S(1)} custom-call(s32[8]{0:T(128)} %freq_hbm.1, s32[5]{0:T(128)} %start_hbm.1, f32[768]{0:T(1024)} %vol_hbm.1, f32[5,96,768]{2,1,0:T(8,128)} %bitcast.9), custom_call_target="tpu_custom_call" | custom-call | tf_op jit(solution)/shard_map/transform/pallas_call | solution.py:100
  3.3 14.2 %all_to_all.16.parts_ref = f32[4,16,3840]{2,1,0:T(8,128)S(1)} all-to-all(f32[4,16,3840]{2,1,0:T(8,128)S(1)} %transform.1), channel_id=1, replica_groups=mesh['cell'=128,'tm'=4] {'tm'}, dimensions={0} | all-to-all | bytes 1966080 | tf_op jit(solution)/shard_map/all_to_all | solution.py:261
  17.5 0.5 %gram.1 = (bf16[96,3840]{1,0:T(8,128)(2,1)S(1)}, f32[128,128]{1,0:T(8,128)S(1)}) custom-call(f32[4,16,3840]{2,1,0:T(8,128)S(1)} %all_to_all.16.parts_ref), custom_call_target="tpu_custom_call" | custom-call | tf_op jit(solution)/shard_map/gram/pallas_call | solution.py:157
  18.0 34.0 %all_to_all.17 = f32[128,1,128]{2,1,0:T(1,128)S(1)} all-to-all(f32[128,1,128]{2,1,0:T(1,128)S(1)} %bitcast.8), channel_id=1, replica_groups=mesh['cell'=128,'tm'=4] {'cell'}, dimensions={0} | all-to-all | bytes 131072 | tf_op jit(solution)/shard_map/all_to_all | solution.py:262
  52.0 1.4 %modes.1 = (f32[10,5,2,768]{3,2,1,0:T(2,128)}, f32[10,2,10]{2,1,0:T(2,128)}) custom-call(f32[128,128]{1,0:T(8,128)S(1)} %bitcast.7, bf16[96,3840]{1,0:T(8,128)(2,1)S(1)} %get-tuple-element.7.stack_ref), custom_call_target="tpu_custom_call" | custom-call | tf_op jit(solution)/shard_map/modes/pallas_call | solution.py:228

commit v5 on v4

--- a/solution.py
+++ b/solution.py
@@ -13,6 +13,8 @@
 COLS = 2 * NB
 SLOTS = NB - 1
 TWO_PI = 6.283185307179586
+TM_ORDER = (2, 3, 0, 1)
+CELL_FIRST = 72
 
 
 def pieces(x):
@@ -60,7 +62,7 @@
     turn = jnp.where(sub >= SLOTS, NFFT // 4, 0)
     rows = []
     for g in range(NF):
-        phase = (freq_ref[g] * tau + turn) & (NFFT - 1)
+        phase = (freq_ref[2 * TM_ORDER[g // 2] + g % 2] * tau + turn) & (NFFT - 1)
         rows.append(hann * jnp.cos(TWO_PI / NFFT * phase.astype(jnp.float32)))
     high, middle, low = pieces(jnp.concatenate(rows, axis=0))
     table_ref[:, 0:tdev] = jnp.concatenate([high, middle, low], axis=0)
@@ -120,13 +122,14 @@
 def gram_kernel(cells, parts_ref, stack_ref, packed_ref):
     sub = lax.broadcasted_iota(jnp.int32, (8, cells), 0)
     full = jnp.zeros((96, 96), jnp.float32)
+    place = [TM_ORDER.index(q) for q in range(4)]
     for v in range(parts_ref.shape[2] // cells):
         at = slice(v * cells, (v + 1) * cells)
         tiles = []
         for f in range(2):
             rows = slice(8 * f, 8 * f + 8)
-            early = parts_ref[0, rows, at] + parts_ref[1, rows, at]
-            late = parts_ref[2, rows, at] + parts_ref[3, rows, at]
+            early = parts_ref[place[0], rows, at] + parts_ref[place[1], rows, at]
+            late = parts_ref[place[2], rows, at] + parts_ref[place[3], rows, at]
             early1 = pltpu.roll(early, 1, 0)
             late1 = pltpu.roll(late, 1, 0)
             late2 = pltpu.roll(late, 2, 0)
@@ -252,14 +255,18 @@
     return jnp.transpose(modes, (2, 0, 1, 3)), jnp.transpose(triangle, (1, 0, 2))
 
 
+def cell_order(count):
+    return [(CELL_FIRST + i) % count for i in range(count)]
+
+
 def on_device(snapshots, volumes, freq_index, block_start):
     return chain(
         snapshots,
         volumes,
         freq_index,
         block_start,
-        lambda x: lax.all_to_all(x, "tm", 0, 0, tiled=True),
-        lambda x: lax.all_to_all(x, "cell", 0, 0, tiled=True),
+        lambda x: lax.all_to_all(x, "tm", 0, 0, tiled=True, axis_index_groups=[list(TM_ORDER)]),
+        lambda x: lax.all_to_all(x, "cell", 0, 0, tiled=True, axis_index_groups=[cell_order(lax.axis_size("cell"))]),
         lax.axis_size("cell"),
     )
 

time: 53.6 us -> 46.7 us (0.87)
  blocking collectives: 48.2 us -> 41.3 us
    all_to_all x2, blocking collectives: 48.2 us -> 41.3 us  [the longest x1 28.6 us: on_device(): lax.all_to_all(x, 'cell', 0, 0, tiled=True, axis_index_groups=[cell_order...]
where the time goes in v5:
time: 46.7 us; the launch traced here: 46.5 us
  blocking collectives  41.3 us (88%)
  Pallas kernels  4.57 us (10%)
  between operations  0.65 us (1%)
    all_to_all x1, blocking collectives, on_device(): lax.all_to_all(x, 'cell', 0, 0, tiled=True, axis_index_groups=[cell_order...  28.6 us
    all_to_all x1, blocking collectives, on_device(): lax.all_to_all(x, 'tm', 0, 0, tiled=True, axis_index_groups=[list(TM_ORDE...  12.7 us
    pallas_call x1, Pallas kernels, transform(): pl.pallas_call(transform_kernel, out_shape=jax.ShapeDtypeStruct((4, 16, n...  2.63 us
    pallas_call x1, Pallas kernels, modes_of(): pl.pallas_call(functools.partial(modes_kernel, nvar * cells * cell_count)...  1.4 us

profile of v5, /device:TPU:1, one launch (start us, length us, event | category | flops | bytes accessed | tf_op | source)
XLA Modules:
  0.0 46.5 jit_solution(3930446295701178755)
XLA Ops:
  0.6 2.6 %transform.1 = f32[4,16,3840]{2,1,0:T(8,128)S(1)} custom-call(s32[8]{0:T(128)} %freq_hbm.1, s32[5]{0:T(128)} %start_hbm.1, f32[768]{0:T(1024)} %vol_hbm.1, f32[5,96,768]{2,1,0:T(8,128)} %bitcast.9), custom_call_target="tpu_custom_call" | custom-call | tf_op jit(solution)/shard_map/transform/pallas_call | solution.py:102
  3.3 12.7 %all_to_all.16.parts_ref = f32[4,16,3840]{2,1,0:T(8,128)S(1)} all-to-all(f32[4,16,3840]{2,1,0:T(8,128)S(1)} %transform.1), channel_id=1, replica_groups={{2,3,0,1},{6,7,4,5},{10,11,8,9},{14,15,12,13},{18,19,16,17},{22,23,20,2..., dimensions={0} | all-to-all | bytes 1966080 | tf_op jit(solution)/shard_map/all_to_all | solution.py:268
  15.9 0.5 %gram.1 = (bf16[96,3840]{1,0:T(8,128)(2,1)S(1)}, f32[128,128]{1,0:T(8,128)S(1)}) custom-call(f32[4,16,3840]{2,1,0:T(8,128)S(1)} %all_to_all.16.parts_ref), custom_call_target="tpu_custom_call" | custom-call | tf_op jit(solution)/shard_map/gram/pallas_call | solution.py:160
  16.5 28.6 %all_to_all.17 = f32[128,1,128]{2,1,0:T(1,128)S(1)} all-to-all(f32[128,1,128]{2,1,0:T(1,128)S(1)} %bitcast.8), channel_id=1, replica_groups={{288,292,296,300,304,308,312,316,320,324,328,332,336,340,344,348,352,35..., dimensions={0} | all-to-all | bytes 131072 | tf_op jit(solution)/shard_map/all_to_all | solution.py:269
  45.1 1.4 %modes.1 = (f32[10,5,2,768]{3,2,1,0:T(2,128)}, f32[10,2,10]{2,1,0:T(2,128)}) custom-call(f32[128,128]{1,0:T(8,128)S(1)} %bitcast.7, bf16[96,3840]{1,0:T(8,128)(2,1)S(1)} %get-tuple-element.7.stack_ref), custom_call_target="tpu_custom_call" | custom-call | tf_op jit(solution)/shard_map/modes/pallas_call | solution.py:231

commit v6 on v5

--- a/solution.py
+++ b/solution.py
@@ -13,8 +13,8 @@
 COLS = 2 * NB
 SLOTS = NB - 1
 TWO_PI = 6.283185307179586
-TM_ORDER = (2, 3, 0, 1)
-CELL_FIRST = 72
+TM_ORDER = (2, 0, 3, 1)
+CELL_FIRST = 89
 
 
 def pieces(x):

time: 46.7 us -> 46.1 us (0.987)
  blocking collectives: 41.3 us -> 40.7 us
    all_to_all x1, blocking collectives: 28.6 us -> 28 us  [on_device(): lax.all_to_all(x, 'cell', 0, 0, tiled=True, axis_index_groups=[cell_order...]
where the time goes in v6:
time: 46.1 us; the launch traced here: 45.9 us
  blocking collectives  40.7 us (88%)
  Pallas kernels  4.57 us (10%)
  between operations  0.65 us (1%)
    all_to_all x1, blocking collectives, on_device(): lax.all_to_all(x, 'cell', 0, 0, tiled=True, axis_index_groups=[cell_order...  28 us
    all_to_all x1, blocking collectives, on_device(): lax.all_to_all(x, 'tm', 0, 0, tiled=True, axis_index_groups=[list(TM_ORDE...  12.7 us
    pallas_call x1, Pallas kernels, transform(): pl.pallas_call(transform_kernel, out_shape=jax.ShapeDtypeStruct((4, 16, n...  2.63 us
    pallas_call x1, Pallas kernels, modes_of(): pl.pallas_call(functools.partial(modes_kernel, nvar * cells * cell_count)...  1.4 us

profile of v6, /device:TPU:1, one launch (start us, length us, event | category | flops | bytes accessed | tf_op | source)
XLA Modules:
  0.0 45.9 jit_solution(8170761435753848304)
XLA Ops:
  0.6 2.6 %transform.1 = f32[4,16,3840]{2,1,0:T(8,128)S(1)} custom-call(s32[8]{0:T(128)} %freq_hbm.1, s32[5]{0:T(128)} %start_hbm.1, f32[768]{0:T(1024)} %vol_hbm.1, f32[5,96,768]{2,1,0:T(8,128)} %bitcast.9), custom_call_target="tpu_custom_call" | custom-call | tf_op jit(solution)/shard_map/transform/pallas_call | solution.py:102
  3.3 12.7 %all_to_all.16.parts_ref = f32[4,16,3840]{2,1,0:T(8,128)S(1)} all-to-all(f32[4,16,3840]{2,1,0:T(8,128)S(1)} %transform.1), channel_id=1, replica_groups={{2,0,3,1},{6,4,7,5},{10,8,11,9},{14,12,15,13},{18,16,19,17},{22,20,23,2..., dimensions={0} | all-to-all | bytes 1966080 | tf_op jit(solution)/shard_map/all_to_all | solution.py:268
  16.0 0.5 %gram.1 = (bf16[96,3840]{1,0:T(8,128)(2,1)S(1)}, f32[128,128]{1,0:T(8,128)S(1)}) custom-call(f32[4,16,3840]{2,1,0:T(8,128)S(1)} %all_to_all.16.parts_ref), custom_call_target="tpu_custom_call" | custom-call | tf_op jit(solution)/shard_map/gram/pallas_call | solution.py:160
  16.5 28.0 %all_to_all.17 = f32[128,1,128]{2,1,0:T(1,128)S(1)} all-to-all(f32[128,1,128]{2,1,0:T(1,128)S(1)} %bitcast.8), channel_id=1, replica_groups={{356,360,364,368,372,376,380,384,388,392,396,400,404,408,412,416,420,42..., dimensions={0} | all-to-all | bytes 131072 | tf_op jit(solution)/shard_map/all_to_all | solution.py:269
  44.5 1.4 %modes.1 = (f32[10,5,2,768]{3,2,1,0:T(2,128)}, f32[10,2,10]{2,1,0:T(2,128)}) custom-call(f32[128,128]{1,0:T(8,128)S(1)} %bitcast.7, bf16[96,3840]{1,0:T(8,128)(2,1)S(1)} %get-tuple-element.7.stack_ref), custom_call_target="tpu_custom_call" | custom-call | tf_op jit(solution)/shard_map/modes/pallas_call | solution.py:231

commit v7 on v6

--- a/solution.py
+++ b/solution.py
@@ -48,22 +48,24 @@
         incoming(v).start()
     quarter = lax.axis_index("tm")
     first = jnp.where(quarter >= 2, 1, 0)
-    sub = lax.broadcasted_iota(jnp.int32, (8, tdev), 0)
-    time = lax.broadcasted_iota(jnp.int32, (8, tdev), 1) + quarter * tdev
+    sub = lax.broadcasted_iota(jnp.int32, (8, NFFT), 0)
+    lane = lax.broadcasted_iota(jnp.int32, (8, NFFT), 1)
+    time = lane + quarter * tdev
+    turns = jnp.cos(TWO_PI / NFFT * lane.astype(jnp.float32))
     slot = sub % SLOTS
     for copy in small:
         copy.wait()
-    start = jnp.zeros((8, tdev), jnp.int32)
+    start = jnp.zeros((8, NFFT), jnp.int32)
     for s in range(SLOTS):
         start = jnp.where(slot == s, start_ref[first + s], start)
     tau = time - start
     valid = (tau >= 0) & (tau < NFFT)
-    hann = jnp.where(valid, 0.5 - 0.5 * jnp.cos(TWO_PI / NFFT * tau.astype(jnp.float32)), 0.0)
+    hann = jnp.where(valid, 0.5 - 0.5 * jnp.take_along_axis(turns, tau & (NFFT - 1), axis=1), 0.0)
     turn = jnp.where(sub >= SLOTS, NFFT // 4, 0)
     rows = []
     for g in range(NF):
         phase = (freq_ref[2 * TM_ORDER[g // 2] + g % 2] * tau + turn) & (NFFT - 1)
-        rows.append(hann * jnp.cos(TWO_PI / NFFT * phase.astype(jnp.float32)))
+        rows.append((hann * jnp.take_along_axis(turns, phase, axis=1))[:, 0:tdev])
     high, middle, low = pieces(jnp.concatenate(rows, axis=0))
     table_ref[:, 0:tdev] = jnp.concatenate([high, middle, low], axis=0)
     table_ref[:, tdev : 2 * tdev] = jnp.concatenate([high, middle, high], axis=0)
@@ -83,17 +85,13 @@
         total = (total[0:64] + (total[64:128] + part)) * root[:, lanes]
         out_ref[:, :, v * cells + low : v * cells + low + 256] = total.reshape(4, 16, 256)
 
-    blocks = tdev // 16
-    tiles = cells // 256
-    for v in range(nvar + 1):
-        if v < nvar:
-            incoming(v).wait()
-        for n in range(tiles):
-            if v < nvar:
-                for r in range(n * blocks // tiles, (n + 1) * blocks // tiles):
-                    split(v, 16 * r)
-            if v > 0:
-                products(v - 1, 256 * n)
+    for v in range(nvar):
+        incoming(v).wait()
+        for low in range(0, tdev, 16):
+            split(v, low)
+    for low in range(0, cells, 256):
+        for v in range(nvar):
+            products(v, low)
 
 
 def transform(snapshots, volumes, freq_index, block_start):

time: 46.1 us -> 45.7 us (level)
  no operation moved by 1% of the time
where the time goes in v7:
time: 45.7 us; the launch traced here: 45.5 us
  blocking collectives  40.7 us (89%)
  Pallas kernels  4.15 us (9%)
  between operations  0.65 us (1%)
    all_to_all x1, blocking collectives, on_device(): lax.all_to_all(x, 'cell', 0, 0, tiled=True, axis_index_groups=[cell_order...  28 us
    all_to_all x1, blocking collectives, on_device(): lax.all_to_all(x, 'tm', 0, 0, tiled=True, axis_index_groups=[list(TM_ORDE...  12.7 us
    pallas_call x1, Pallas kernels, transform(): pl.pallas_call(transform_kernel, out_shape=jax.ShapeDtypeStruct((4, 16, n...  2.21 us
    pallas_call x1, Pallas kernels, modes_of(): pl.pallas_call(functools.partial(modes_kernel, nvar * cells * cell_count)...  1.4 us

profile of v7, /device:TPU:1, one launch (start us, length us, event | category | flops | bytes accessed | tf_op | source)
XLA Modules:
  0.0 45.5 jit_solution(10858759487979140032)
XLA Ops:
  0.6 2.2 %transform.1 = f32[4,16,3840]{2,1,0:T(8,128)S(1)} custom-call(s32[8]{0:T(128)} %freq_hbm.1, s32[5]{0:T(128)} %start_hbm.1, f32[768]{0:T(1024)} %vol_hbm.1, f32[5,96,768]{2,1,0:T(8,128)} %bitcast.9), custom_call_target="tpu_custom_call" | custom-call | tf_op jit(solution)/shard_map/transform/pallas_call | solution.py:100
  2.8 12.7 %all_to_all.16.parts_ref = f32[4,16,3840]{2,1,0:T(8,128)S(1)} all-to-all(f32[4,16,3840]{2,1,0:T(8,128)S(1)} %transform.1), channel_id=1, replica_groups={{2,0,3,1},{6,4,7,5},{10,8,11,9},{14,12,15,13},{18,16,19,17},{22,20,23,2..., dimensions={0} | all-to-all | bytes 1966080 | tf_op jit(solution)/shard_map/all_to_all | solution.py:266
  15.5 0.5 %gram.1 = (bf16[96,3840]{1,0:T(8,128)(2,1)S(1)}, f32[128,128]{1,0:T(8,128)S(1)}) custom-call(f32[4,16,3840]{2,1,0:T(8,128)S(1)} %all_to_all.16.parts_ref), custom_call_target="tpu_custom_call" | custom-call | tf_op jit(solution)/shard_map/gram/pallas_call | solution.py:158
  16.1 28.0 %all_to_all.17 = f32[128,1,128]{2,1,0:T(1,128)S(1)} all-to-all(f32[128,1,128]{2,1,0:T(1,128)S(1)} %bitcast.8), channel_id=1, replica_groups={{356,360,364,368,372,376,380,384,388,392,396,400,404,408,412,416,420,42..., dimensions={0} | all-to-all | bytes 131072 | tf_op jit(solution)/shard_map/all_to_all | solution.py:267
  44.1 1.4 %modes.1 = (f32[10,5,2,768]{3,2,1,0:T(2,128)}, f32[10,2,10]{2,1,0:T(2,128)}) custom-call(f32[128,128]{1,0:T(8,128)S(1)} %bitcast.7, bf16[96,3840]{1,0:T(8,128)(2,1)S(1)} %get-tuple-element.7.stack_ref), custom_call_target="tpu_custom_call" | custom-call | tf_op jit(solution)/shard_map/modes/pallas_call | solution.py:229

commit v8 on v7

--- a/solution.py
+++ b/solution.py
@@ -13,8 +13,8 @@
 COLS = 2 * NB
 SLOTS = NB - 1
 TWO_PI = 6.283185307179586
-TM_ORDER = (2, 0, 3, 1)
-CELL_FIRST = 89
+TM_ORDER = (2, 1, 3, 0)
+CELL_FIRST = 105
 
 
 def pieces(x):

time: 45.7 us -> 45.5 us (level)
  no operation moved by 1% of the time
where the time goes in v8:
time: 45.5 us; the launch traced here: 45.4 us
  blocking collectives  40.6 us (89%)
  Pallas kernels  4.15 us (9%)
  between operations  0.65 us (1%)
    all_to_all x1, blocking collectives, on_device(): lax.all_to_all(x, 'cell', 0, 0, tiled=True, axis_index_groups=[cell_order...  27.8 us
    all_to_all x1, blocking collectives, on_device(): lax.all_to_all(x, 'tm', 0, 0, tiled=True, axis_index_groups=[list(TM_ORDE...  12.7 us
    pallas_call x1, Pallas kernels, transform(): pl.pallas_call(transform_kernel, out_shape=jax.ShapeDtypeStruct((4, 16, n...  2.21 us
    pallas_call x1, Pallas kernels, modes_of(): pl.pallas_call(functools.partial(modes_kernel, nvar * cells * cell_count)...  1.4 us

profile of v8, /device:TPU:1, one launch (start us, length us, event | category | flops | bytes accessed | tf_op | source)
XLA Modules:
  0.0 45.4 jit_solution(18005626644329544370)
XLA Ops:
  0.6 2.2 %transform.1 = f32[4,16,3840]{2,1,0:T(8,128)S(1)} custom-call(s32[8]{0:T(128)} %freq_hbm.1, s32[5]{0:T(128)} %start_hbm.1, f32[768]{0:T(1024)} %vol_hbm.1, f32[5,96,768]{2,1,0:T(8,128)} %bitcast.9), custom_call_target="tpu_custom_call" | custom-call | tf_op jit(solution)/shard_map/transform/pallas_call | solution.py:100
  2.8 12.7 %all_to_all.16.parts_ref = f32[4,16,3840]{2,1,0:T(8,128)S(1)} all-to-all(f32[4,16,3840]{2,1,0:T(8,128)S(1)} %transform.1), channel_id=1, replica_groups={{2,1,3,0},{6,5,7,4},{10,9,11,8},{14,13,15,12},{18,17,19,16},{22,21,23,2..., dimensions={0} | all-to-all | bytes 1966080 | tf_op jit(solution)/shard_map/all_to_all | solution.py:266
  15.6 0.5 %gram.1 = (bf16[96,3840]{1,0:T(8,128)(2,1)S(1)}, f32[128,128]{1,0:T(8,128)S(1)}) custom-call(f32[4,16,3840]{2,1,0:T(8,128)S(1)} %all_to_all.16.parts_ref), custom_call_target="tpu_custom_call" | custom-call | tf_op jit(solution)/shard_map/gram/pallas_call | solution.py:158
  16.1 27.8 %all_to_all.17 = f32[128,1,128]{2,1,0:T(1,128)S(1)} all-to-all(f32[128,1,128]{2,1,0:T(1,128)S(1)} %bitcast.8), channel_id=1, replica_groups={{420,424,428,432,436,440,444,448,452,456,460,464,468,472,476,480,484,48..., dimensions={0} | all-to-all | bytes 131072 | tf_op jit(solution)/shard_map/all_to_all | solution.py:267
  44.0 1.4 %modes.1 = (f32[10,5,2,768]{3,2,1,0:T(2,128)}, f32[10,2,10]{2,1,0:T(2,128)}) custom-call(f32[128,128]{1,0:T(8,128)S(1)} %bitcast.7, bf16[96,3840]{1,0:T(8,128)(2,1)S(1)} %get-tuple-element.7.stack_ref), custom_call_target="tpu_custom_call" | custom-call | tf_op jit(solution)/shard_map/modes/pallas_call | solution.py:229

commit v9 on v8

--- a/solution.py
+++ b/solution.py
@@ -14,7 +14,7 @@
 SLOTS = NB - 1
 TWO_PI = 6.283185307179586
 TM_ORDER = (2, 1, 3, 0)
-CELL_FIRST = 105
+CELL_FIRST = 89
 
 
 def pieces(x):

time: 45.5 us -> 45.7 us (level)
  no operation moved by 1% of the time
where the time goes in v9:
time: 45.7 us; the launch traced here: 45.5 us
  blocking collectives  40.7 us (89%)
  Pallas kernels  4.15 us (9%)
  between operations  0.65 us (1%)
    all_to_all x1, blocking collectives, on_device(): lax.all_to_all(x, 'cell', 0, 0, tiled=True, axis_index_groups=[cell_order...  28 us
    all_to_all x1, blocking collectives, on_device(): lax.all_to_all(x, 'tm', 0, 0, tiled=True, axis_index_groups=[list(TM_ORDE...  12.7 us
    pallas_call x1, Pallas kernels, transform(): pl.pallas_call(transform_kernel, out_shape=jax.ShapeDtypeStruct((4, 16, n...  2.21 us
    pallas_call x1, Pallas kernels, modes_of(): pl.pallas_call(functools.partial(modes_kernel, nvar * cells * cell_count)...  1.4 us

profile of v9, /device:TPU:1, one launch (start us, length us, event | category | flops | bytes accessed | tf_op | source)
XLA Modules:
  0.0 45.5 jit_solution(10444219011354596383)
XLA Ops:
  0.6 2.2 %transform.1 = f32[4,16,3840]{2,1,0:T(8,128)S(1)} custom-call(s32[8]{0:T(128)} %freq_hbm.1, s32[5]{0:T(128)} %start_hbm.1, f32[768]{0:T(1024)} %vol_hbm.1, f32[5,96,768]{2,1,0:T(8,128)} %bitcast.9), custom_call_target="tpu_custom_call" | custom-call | tf_op jit(solution)/shard_map/transform/pallas_call | solution.py:100
  2.8 12.7 %all_to_all.16.parts_ref = f32[4,16,3840]{2,1,0:T(8,128)S(1)} all-to-all(f32[4,16,3840]{2,1,0:T(8,128)S(1)} %transform.1), channel_id=1, replica_groups={{2,1,3,0},{6,5,7,4},{10,9,11,8},{14,13,15,12},{18,17,19,16},{22,21,23,2..., dimensions={0} | all-to-all | bytes 1966080 | tf_op jit(solution)/shard_map/all_to_all | solution.py:266
  15.6 0.5 %gram.1 = (bf16[96,3840]{1,0:T(8,128)(2,1)S(1)}, f32[128,128]{1,0:T(8,128)S(1)}) custom-call(f32[4,16,3840]{2,1,0:T(8,128)S(1)} %all_to_all.16.parts_ref), custom_call_target="tpu_custom_call" | custom-call | tf_op jit(solution)/shard_map/gram/pallas_call | solution.py:158
  16.1 28.0 %all_to_all.17 = f32[128,1,128]{2,1,0:T(1,128)S(1)} all-to-all(f32[128,1,128]{2,1,0:T(1,128)S(1)} %bitcast.8), channel_id=1, replica_groups={{356,360,364,368,372,376,380,384,388,392,396,400,404,408,412,416,420,42..., dimensions={0} | all-to-all | bytes 131072 | tf_op jit(solution)/shard_map/all_to_all | solution.py:267
  44.1 1.4 %modes.1 = (f32[10,5,2,768]{3,2,1,0:T(2,128)}, f32[10,2,10]{2,1,0:T(2,128)}) custom-call(f32[128,128]{1,0:T(8,128)S(1)} %bitcast.7, bf16[96,3840]{1,0:T(8,128)(2,1)S(1)} %get-tuple-element.7.stack_ref), custom_call_target="tpu_custom_call" | custom-call | tf_op jit(solution)/shard_map/modes/pallas_call | solution.py:229
